TPU v7x, 512 devices: a whole 4x8x8 slice. The times are simulated.
512 devices in a mesh: grp: 32 (over x, z), voc: 16 (over y, core).
Axes of the slice: x: 4, y: 8, z: 8, core: 2. Of those that a mesh axis runs over, the one named last changes fastest.
Arguments:
- hidden: bfloat16 [24576, 4096], P('grp', 'voc'), may hold values from -50 to 50
- targets: int32 [24576], P('grp'), may hold values from 0 to 15999
- row_count: int32 [32], P('grp'), may hold values from 96 to 768, as said below
- norm_gain: bfloat16 [4096], replicated, may hold values from 0.099609375 to 1.8984375
- head_weight: bfloat16 [4096, 16000], P('grp', 'voc'), may hold values from -0.71 to 0.71
- return_from: int32 [24576], P('grp'), may hold values from 0 to 24575, each once
Outputs:
- token_logp: float32 [24576], P('grp')
- token_entropy: float32 [24576], P('grp')
Inputs may be any that keep to these rules, and one draw needn't show every extreme that they name: `row_count`: the live rows of a group are its first ones. `return_from`: every slot index appears once.
All inputs are finite; a program needn't handle non-finite values.
Results may differ from a plain program's by a relative error of at most 0.0088.
Values may be sent and summed in bfloat16 or wider, within the bound.
A program may use at most 64 MiB of HBM per device.

v0:
```python
import jax
import jax.numpy as jnp
from jax import lax
from jax.sharding import PartitionSpec as P

BLOCK = 128


EPSILON = 1e-05


def normalize(raw, norm_gain):
    values = raw.astype(jnp.float32)
    scale = lax.rsqrt(jnp.mean(values * values, axis=1, keepdims=True) + EPSILON)
    return (values * scale * norm_gain.astype(jnp.float32)[None, :]).astype(jnp.bfloat16)


def local(hidden, targets, row_count, norm_gain, head_weight, return_from):
    tok_rows = hidden.shape[0]
    block_count = tok_rows // BLOCK
    positions = jnp.arange(tok_rows, dtype=jnp.int32)
    live_rows = positions < row_count[0]
    block_live = [block * BLOCK < row_count[0] for block in range(block_count)]
    full_rows = lax.all_gather(hidden, "voc", axis=1, tiled=True)
    normed = normalize(full_rows, norm_gain)
    vocab_local = head_weight.shape[1]
    piece = lax.all_gather(head_weight, "grp", axis=0, tiled=True)
    terms = []
    for block in range(block_count):
        section = normed[block * BLOCK : (block + 1) * BLOCK]
        terms.append(
            lax.cond(
                block_live[block],
                lambda inner: jnp.dot(inner, piece, preferred_element_type=jnp.float32),
                lambda inner: jnp.zeros((inner.shape[0], piece.shape[1]), jnp.float32),
                section,
            )
        )
    logits = jnp.concatenate(terms, 0)
    peak = jnp.max(logits, axis=1)
    shifted = jnp.exp(logits - peak[:, None])
    total = jnp.sum(shifted, axis=1)
    weighted = jnp.sum(shifted * logits, axis=1)
    global_columns = lax.axis_index("voc") * vocab_local + jnp.arange(vocab_local, dtype=jnp.int32)
    picked = jnp.sum(jnp.where(global_columns[None, :] == targets[:, None], logits, 0.0), axis=1)
    peak_all = lax.pmax(peak, "voc")
    factor = jnp.exp(peak - peak_all)
    total_all, weighted_all, picked_all = lax.psum(
        (total * factor, weighted * factor, picked), "voc"
    )
    log_total = peak_all + jnp.log(total_all)
    logp = jnp.where(live_rows, picked_all - log_total, 0.0)
    entropy = jnp.where(live_rows, log_total - weighted_all / total_all, 0.0)
    every_logp, every_entropy = (
        lax.all_gather(logp, "grp", axis=0, tiled=True),
        lax.all_gather(entropy, "grp", axis=0, tiled=True),
    )
    return (jnp.take(every_logp, return_from, axis=0), jnp.take(every_entropy, return_from, axis=0))


def solution(mesh):
    placed = (P("grp", "voc"), P("grp"), P("grp"), P(), P("grp", "voc"), P("grp"))
    return jax.shard_map(
        local, mesh=mesh, in_specs=placed, out_specs=(P("grp"), P("grp")), check_vma=False
    )
```

profile of v0, /device:TPU:4, one launch (start us, length us, event | category | flops | bytes accessed | tf_op | source)
XLA Modules:
  0.0 404.6 jit_solution(3456928041768944532)
XLA Ops:
  7.2 0.0 all-gather.5.cloned.1.call-start
  7.2 0.7 all-gather.5.cloned.1.call-update
  7.9 0.0 all-gather.7.cloned.1.call-start
  7.9 1.8 copy.10
  9.8 0.0 all-gather.7.cloned.1.call-update
  10.5 0.7 convert_element_type.29
  11.2 0.7 compare_select_fusion
  11.9 61.6 %all-gather.5.cloned.1.call-done = bf16[768,4096]{1,0:T(8,128)(2,1)} async-done(((bf16[768,256]{1,0:T(8,128)(2,1)}), bf16[768,4096]{1,0:T(8,128)(2,1)}) %all-gather.5.cloned.1.call-update) | async-done | bytes 6291472 | tf_op jit(solution)/shard_map/all_gather | solution.py:24
  73.5 0.0 copy-start
  73.5 4.2 %fusion.12 = f32[768]{0:T(1024)S(1)} fusion(bf16[768,4096]{1,0:T(8,128)(2,1)} %all-gather.5.cloned.1.call-done), kind=kLoop, calls=%fused_computation.16 | loop fusion | flops 9436416 | bytes 6294528 | tf_op jit(solution)/shard_map/reduce_sum | solution.py:14
  77.8 0.4 copy-done
  78.1 5.4 %fusion.14 = bf16[768,4096]{1,0:T(8,128)(2,1)} fusion(bf16[768,4096]{1,0:T(8,128)(2,1)S(1)} %copy-done, f32[4096]{0:T(1024)S(1)} %convert_element_type.29, f32[768]{0:T(1024)S(1)} %add_rsqrt_fusion), kind=kLoop, calls=%fused_computation.18 | loop fusion | flops 12582912 | bytes 12602368 | tf_op jit(solution)/shard_map/convert_element_type | solution.py:15
  83.5 94.8 %all-gather.7.cloned.1.call-done = bf16[4096,1000]{1,0:T(8,128)(2,1)} async-done(((bf16[128,1000]{1,0:T(8,128)(2,1)}), bf16[4096,1000]{1,0:T(8,128)(2,1)}) %all-gather.7.cloned.1.call-update) | async-done | bytes 8192016 | tf_op jit(solution)/shard_map/all_gather | solution.py:27
  178.3 7.1 %conditional.6 = (f32[128,1000]{0,1:T(8,128)S(1)}) conditional(s32[]{:T(128)} %convert_element_type.27, () %tuple.45, (bf16[768,4096]{1,0:T(8,128)(2,1)}, bf16[4096,1000]{1,0:T(8,128)(2,1)}) %tuple.46), branch_computations={%region_1.0_spmd, %region_2.0_spmd} | conditional | flops 1048576000 | bytes 9949192 | solution.py:32
  178.3 7.1 %fusion = f32[128,1000]{0,1:T(8,128)S(1)} fusion(bf16[4096,1000]{1,0:T(8,128)(2,1)} %get-tuple-element.50, bf16[768,4096]{1,0:T(8,128)(2,1)} %get-tuple-element.48), kind=kOutput, calls=%fused_computation.2 | convolution fusion | flops 1048576000 | bytes 9949184 | tf_op jit(solution)/shard_map/cond/branch_1_fun/dot_general | solution.py:34
  185.4 0.0 copy-start.1
  185.4 0.8 copy-done.1
  186.2 1.1 constant_dynamic-update-slice_fusion.5
  187.3 7.9 %conditional.11 = (f32[128,1000]{0,1:T(8,128)}) conditional(s32[]{:T(128)} %convert_element_type.35, () %tuple.51, (bf16[768,4096]{1,0:T(8,128)(2,1)}, bf16[4096,1000]{1,0:T(8,128)(2,1)}) %tuple.46), branch_computations={%region_11.0_spmd, %region_12.0_spmd} | conditional | flops 1048576000 | bytes 9949192 | solution.py:32
  187.3 7.8 %fusion.10 = f32[128,1000]{0,1:T(8,128)} fusion(bf16[4096,1000]{1,0:T(8,128)(2,1)} %get-tuple-element.60, bf16[768,4096]{1,0:T(8,128)(2,1)} %get-tuple-element.59), kind=kOutput, calls=%fused_computation.12 | convolution fusion | flops 1048576000 | bytes 9949184 | tf_op jit(solution)/shard_map/cond/branch_1_fun/dot_general | solution.py:34
  195.1 7.9 %conditional.10 = (f32[128,1000]{0,1:T(8,128)}) conditional(s32[]{:T(128)} %convert_element_type.34, () %tuple.50, (bf16[768,4096]{1,0:T(8,128)(2,1)}, bf16[4096,1000]{1,0:T(8,128)(2,1)}) %tuple.46), branch_computations={%region_9.0_spmd, %region_10.0_spmd} | conditional | flops 1048576000 | bytes 9949192 | solution.py:32
  195.1 7.9 %fusion.8 = f32[128,1000]{0,1:T(8,128)} fusion(bf16[4096,1000]{1,0:T(8,128)(2,1)} %get-tuple-element.58, bf16[768,4096]{1,0:T(8,128)(2,1)} %get-tuple-element.57), kind=kOutput, calls=%fused_computation.10 | convolution fusion | flops 1048576000 | bytes 9949184 | tf_op jit(solution)/shard_map/cond/branch_1_fun/dot_general | solution.py:34
  203.0 7.8 %conditional.9 = (f32[128,1000]{0,1:T(8,128)}) conditional(s32[]{:T(128)} %convert_element_type.33, () %tuple.49, (bf16[768,4096]{1,0:T(8,128)(2,1)}, bf16[4096,1000]{1,0:T(8,128)(2,1)}) %tuple.46), branch_computations={%region_7.0_spmd, %region_8.0_spmd} | conditional | flops 1048576000 | bytes 9949192 | solution.py:32
  203.0 7.8 %fusion.6 = f32[128,1000]{0,1:T(8,128)} fusion(bf16[4096,1000]{1,0:T(8,128)(2,1)} %get-tuple-element.56, bf16[768,4096]{1,0:T(8,128)(2,1)} %get-tuple-element.55), kind=kOutput, calls=%fused_computation.8 | convolution fusion | flops 1048576000 | bytes 9949184 | tf_op jit(solution)/shard_map/cond/branch_1_fun/dot_general | solution.py:34
  210.8 7.9 %conditional.8 = (f32[128,1000]{0,1:T(8,128)}) conditional(s32[]{:T(128)} %convert_element_type.32, () %tuple.48, (bf16[768,4096]{1,0:T(8,128)(2,1)}, bf16[4096,1000]{1,0:T(8,128)(2,1)}) %tuple.46), branch_computations={%region_5.0_spmd, %region_6.0_spmd} | conditional | flops 1048576000 | bytes 9949192 | solution.py:32
  210.8 7.9 %fusion.4 = f32[128,1000]{0,1:T(8,128)} fusion(bf16[4096,1000]{1,0:T(8,128)(2,1)} %get-tuple-element.54, bf16[768,4096]{1,0:T(8,128)(2,1)} %get-tuple-element.53), kind=kOutput, calls=%fused_computation.6 | convolution fusion | flops 1048576000 | bytes 9949184 | tf_op jit(solution)/shard_map/cond/branch_1_fun/dot_general | solution.py:34
  218.7 7.9 %conditional.7 = (f32[128,1000]{0,1:T(8,128)}) conditional(s32[]{:T(128)} %convert_element_type.31, () %tuple.47, (bf16[768,4096]{1,0:T(8,128)(2,1)}, bf16[4096,1000]{1,0:T(8,128)(2,1)}) %tuple.46), branch_computations={%region_3.0_spmd, %region_4.0_spmd} | conditional | flops 1048576000 | bytes 9949192 | solution.py:32
  218.7 7.9 %fusion.2 = f32[128,1000]{0,1:T(8,128)} fusion(bf16[4096,1000]{1,0:T(8,128)(2,1)} %get-tuple-element.52, bf16[768,4096]{1,0:T(8,128)(2,1)} %get-tuple-element.51), kind=kOutput, calls=%fused_computation.4 | convolution fusion | flops 1048576000 | bytes 9949184 | tf_op jit(solution)/shard_map/cond/branch_1_fun/dot_general | solution.py:34
  226.6 0.0 copy-start.3
  226.6 1.1 constant_dynamic-update-slice_fusion.4
  227.7 1.1 constant_dynamic-update-slice_fusion.3
  228.8 1.1 constant_dynamic-update-slice_fusion.2
  229.9 0.0 copy-start.2
  229.9 1.1 constant_dynamic-update-slice_fusion.1
  231.0 1.1 constant_dynamic-update-slice_fusion
  232.0 0.2 reduce_max.9
  232.3 25.4 %pmax.7 = f32[768]{0:T(1024)S(1)} all-reduce(f32[768]{0:T(1024)S(1)} %reduce_max.9), channel_id=1, replica_groups=mesh['grp'=32,'voc'=16] {'voc'}, use_global_device_ids=true, to_apply=%region_16.17 | all-reduce | flops 768 | bytes 6144 | tf_op jit(solution)/shard_map/pmax | solution.py:46
  257.7 0.0 copy-done.3
  257.7 1.4 multiply_reduce_fusion
  259.1 45.7 %all-reduce = (f32[768]{0:T(1024)S(1)}, f32[768]{0:T(1024)S(1)}, f32[768]{0:T(1024)S(1)}) all-reduce(f32[768]{0:T(1024)S(1)} %get-tuple-element.65, f32[768]{0:T(1024)S(1)} %get-tuple-element.74, f32[768]{0:T(1024)S(1)} %get-tuple-element.73), channel_id=1, replica_groups=mesh['grp'=32,'voc'=16] {'voc'}, use_global_device_ids=true, to_apply=%region_14.0 | all-reduce | flops 2304 | bytes 18432 | tf_op jit(solution)/shard_map/psum | solution.py:48
  304.8 39.8 %all-gather.1 = f32[32,1,768]{2,1,0:T(1,128)S(1)} all-gather(f32[1,1,768]{2,1,0:T(1,128)S(1)} %reshape.44), channel_id=1, replica_groups=mesh['grp'=32,'voc'=16] {'grp'}, dimensions={0}, use_global_device_ids=true | all-gather | bytes 101376 | tf_op jit(solution)/shard_map/all_gather | solution.py:56
  344.6 4.5 %gather_fusion.1 = f32[768]{0:T(1024)S(1)} fusion(f32[24576]{0:T(1024)S(1)} %bitcast.17, s32[1024]{0:T(1024)S(1)} %pad_clamp_fusion), kind=kCustom, calls=%fused_computation.1.clone | custom fusion | bytes 9216 | tf_op jit(solution)/shard_map/jit(_take)/gather | solution.py:58
  349.0 0.0 copy-done.2
  349.0 0.6 broadcast_select_fusion
  349.6 43.0 %all-gather = f32[32,1,768]{2,1,0:T(1,128)S(1)} all-gather(f32[1,1,768]{2,1,0:T(1,128)S(1)} %reshape.42), channel_id=1, replica_groups=mesh['grp'=32,'voc'=16] {'grp'}, dimensions={0}, use_global_device_ids=true | all-gather | bytes 101376 | tf_op jit(solution)/shard_map/all_gather | solution.py:55
  392.7 4.5 %gather_fusion = f32[768]{0:T(1024)S(1)} fusion(f32[24576]{0:T(1024)S(1)} %bitcast.16, s32[1024]{0:T(1024)S(1)} %pad_clamp_fusion), kind=kCustom, calls=%fused_computation.clone | custom fusion | bytes 9216 | tf_op jit(solution)/shard_map/jit(_take)/gather | solution.py:58
  397.1 0.6 broadcast_select_fusion.1
  (7 shorter events, 0.0 us)
Async XLA Ops:
  7.2 66.4 %all-gather.5.cloned.1.call-start = ((), (), s32[]{:S(2)}) async-start(), calls=%async_computation | async-start | bytes 6684672 | tf_op jit(solution)/shard_map/all_gather | solution.py:24
  7.9 170.4 %all-gather.7.cloned.1.call-start = ((), (), s32[]{:S(2)}) async-start(), calls=%async_computation.1 | async-start | bytes 8650752 | tf_op jit(solution)/shard_map/all_gather | solution.py:27
  73.5 4.6 %copy-start = (bf16[768,4096]{1,0:T(8,128)(2,1)S(1)}, bf16[768,4096]{1,0:T(8,128)(2,1)}, u32[]{:S(2)}) copy-start(bf16[768,4096]{1,0:T(8,128)(2,1)} %all-gather.5.cloned.1.call-done) | copy-start | bytes 18874372
  185.4 0.8 copy-start.1
  226.6 31.1 %copy-start.3 = (s32[768]{0:T(1024)S(1)}, s32[768]{0:T(1024)}, u32[]{:S(2)}) copy-start(s32[768]{0:T(1024)} %param.21) | copy-start | bytes 9220
  229.9 119.2 %copy-start.2 = (s32[768]{0:T(1024)S(1)}, s32[768]{0:T(1024)}, u32[]{:S(2)}) copy-start(s32[768]{0:T(1024)} %param.25) | copy-start | bytes 9220
Sparse Core Ops, SparseCore 0:
  10.0 63.4 all-gather.4
  76.7 101.5 all-gather.6
where the time goes:
time: 405 us
  waiting for transfers between devices  157 us (39%)
  blocking collectives  154 us (38%)
  matrix products  46.4 us (11%)
  local copies, waits for them, and re-layouts  18.4 us (5%)
  between operations  14.8 us (4%)
  other arithmetic  13.9 us (3%)
    all_gather x1, waiting for transfers between devices, local(): piece = lax.all_gather(head_weight, 'grp', axis=0, tiled=True)  94.8 us
    all_gather x1, waiting for transfers between devices, local(): full_rows = lax.all_gather(hidden, 'voc', axis=1, tiled=True)  61.6 us
    dot_general x6, matrix products, local(): jnp.dot(inner, piece, preferred_element_type=jnp.float32)  46.4 us
    psum x1, blocking collectives, local(): lax.psum((total * factor, weighted * factor, picked), 'voc')  45.7 us
    all_gather x1, blocking collectives, local(): lax.all_gather(logp, 'grp', axis=0, tiled=True)  43 us
    all_gather x1, blocking collectives, local(): lax.all_gather(entropy, 'grp', axis=0, tiled=True)  39.8 us
    pmax x1, blocking collectives, local(): peak_all = lax.pmax(peak, 'voc')  25.4 us
    unnamed x16, local copies, waits for them, and re-layouts  8.41 us
  transfers between devices with their start and end apart: 2, of which 2 were waited for; matrix products, arithmetic and copies ran while one was open for 3% of the time, Pallas kernels for 0%

commit v1 on v0

v1 whole, which is shorter than its diff:
```python
import functools

import jax
import jax.numpy as jnp
from jax import lax
from jax.experimental import pallas as pl
from jax.experimental.pallas import tpu as pltpu
from jax.sharding import PartitionSpec as P

MESH = pl.DeviceIdType.MESH

EPSILON = 1e-05


def normalize(raw, norm_gain):
    values = raw.astype(jnp.float32)
    scale = lax.rsqrt(jnp.mean(values * values, axis=1, keepdims=True) + EPSILON)
    return (values * scale * norm_gain.astype(jnp.float32)[None, :]).astype(jnp.bfloat16)


def _share_kernel(axis, other, n, x_ref, o_ref, send_sem, recv_sem):
    me = lax.axis_index(axis)
    fixed = lax.axis_index(other)

    def dev(t):
        return (fixed, t) if axis == "voc" else (t, fixed)

    barrier = pltpu.get_barrier_semaphore()
    for k in range(1, n):
        pl.semaphore_signal(barrier, inc=1, device_id=dev(lax.rem(me + k, n)), device_id_type=MESH)
    pl.semaphore_wait(barrier, n - 1)
    copies = []
    for k in range(1, n):
        copy = pltpu.make_async_remote_copy(
            src_ref=x_ref,
            dst_ref=o_ref.at[pl.ds(me, 1)],
            send_sem=send_sem.at[k],
            recv_sem=recv_sem.at[k],
            device_id=dev(lax.rem(me + k, n)),
            device_id_type=MESH,
        )
        copy.start()
        copies.append(copy)
    o_ref[pl.ds(me, 1), :] = x_ref[...]
    for k in range(1, n):
        source = lax.rem(me + n - k, n)
        incoming = pltpu.make_async_remote_copy(
            src_ref=x_ref,
            dst_ref=o_ref.at[pl.ds(source, 1)],
            send_sem=send_sem.at[k],
            recv_sem=recv_sem.at[k],
            device_id=dev(source),
            device_id_type=MESH,
        )
        copies[k - 1].wait_send()
        incoming.wait_recv()


def share(row, axis, other, n, collective_id):
    width = row.shape[1]
    return pl.pallas_call(
        functools.partial(_share_kernel, axis, other, n),
        out_shape=jax.ShapeDtypeStruct((n, width), row.dtype),
        in_specs=[pl.BlockSpec(memory_space=pltpu.VMEM)],
        out_specs=pl.BlockSpec(memory_space=pltpu.VMEM),
        scratch_shapes=[pltpu.SemaphoreType.DMA((n,)), pltpu.SemaphoreType.DMA((n,))],
        compiler_params=pltpu.CompilerParams(collective_id=collective_id, has_side_effects=True),
    )(row)


def local(hidden, targets, row_count, norm_gain, head_weight, return_from, *, n_voc, n_grp):
    tok_rows = hidden.shape[0]
    positions = jnp.arange(tok_rows, dtype=jnp.int32)
    live_rows = positions < row_count[0]
    full_rows = lax.all_gather(hidden, "voc", axis=1, tiled=True)
    normed = normalize(full_rows, norm_gain)
    vocab_local = head_weight.shape[1]
    piece = lax.all_gather(head_weight, "grp", axis=0, tiled=True)
    logits = jnp.dot(normed, piece, preferred_element_type=jnp.float32)
    peak = jnp.max(logits, axis=1)
    shifted = jnp.exp(logits - peak[:, None])
    total = jnp.sum(shifted, axis=1)
    weighted = jnp.sum(shifted * logits, axis=1)
    global_columns = lax.axis_index("voc") * vocab_local + jnp.arange(vocab_local, dtype=jnp.int32)
    picked = jnp.sum(jnp.where(global_columns[None, :] == targets[:, None], logits, 0.0), axis=1)
    stats = jnp.concatenate([peak, total, weighted, picked])[None, :]
    parts = share(stats, "voc", "grp", n_voc, 0).reshape(n_voc, 4, tok_rows)
    peaks, totals, weights, picks = parts[:, 0], parts[:, 1], parts[:, 2], parts[:, 3]
    peak_all = jnp.max(peaks, axis=0)
    factor = jnp.exp(peaks - peak_all[None, :])
    total_all = jnp.sum(totals * factor, axis=0)
    weighted_all = jnp.sum(weights * factor, axis=0)
    picked_all = jnp.sum(picks, axis=0)
    log_total = peak_all + jnp.log(total_all)
    logp = jnp.where(live_rows, picked_all - log_total, 0.0)
    entropy = jnp.where(live_rows, log_total - weighted_all / total_all, 0.0)
    results = share(jnp.concatenate([logp, entropy])[None, :], "grp", "voc", n_grp, 1)
    results = results.reshape(n_grp, 2, tok_rows)
    every_logp = results[:, 0].reshape(n_grp * tok_rows)
    every_entropy = results[:, 1].reshape(n_grp * tok_rows)
    return (jnp.take(every_logp, return_from, axis=0), jnp.take(every_entropy, return_from, axis=0))


def solution(mesh):
    placed = (P("grp", "voc"), P("grp"), P("grp"), P(), P("grp", "voc"), P("grp"))
    body = functools.partial(local, n_voc=mesh.shape["voc"], n_grp=mesh.shape["grp"])
    return jax.shard_map(
        body, mesh=mesh, in_specs=placed, out_specs=(P("grp"), P("grp")), check_vma=False
    )
```

time: 405 us -> 247 us (0.61)
  the two profiles are of different devices: /device:TPU:4 before, /device:TPU:1 now
where the time goes in v1:
time: 247 us; the launch traced here: 246 us
  waiting for transfers between devices  169 us (68%)
  Pallas kernels  30.7 us (12%)
  between operations  14.8 us (6%)
  local copies, waits for them, and re-layouts  11.7 us (5%)
  matrix products  11.2 us (5%)
  other arithmetic  8.87 us (4%)
    all_gather x1, waiting for transfers between devices, local(): piece = lax.all_gather(head_weight, 'grp', axis=0, tiled=True)  103 us
    all_gather x1, waiting for transfers between devices, local(): full_rows = lax.all_gather(hidden, 'voc', axis=1, tiled=True)  64.2 us
    pallas_call x2, Pallas kernels, share(): pl.pallas_call(functools.partial(_share_kernel, axis, other, n), out_shap...  30.7 us
    dot_general x1, matrix products, local(): logits = jnp.dot(normed, piece, preferred_element_type=jnp.float32)  11.2 us
  transfers between devices with their start and end apart: 2, of which 2 were waited for; matrix products, arithmetic and copies ran while one was open for 2% of the time, Pallas kernels for 0%

profile of v1, /device:TPU:1, one launch (start us, length us, event | category | flops | bytes accessed | tf_op | source)
XLA Modules:
  0.0 246.2 jit_solution(13325115162928460834)
XLA Ops:
  7.2 0.0 all-gather.3.cloned.1.call-start
  7.2 0.7 all-gather.3.cloned.1.call-update
  7.9 0.0 all-gather.5.cloned.1.call-start
  7.9 0.7 all-gather.5.cloned.1.call-update
  8.7 0.7 convert_element_type.10
  10.0 0.7 compare_select_fusion
  10.7 64.2 %all-gather.3.cloned.1.call-done = bf16[768,4096]{1,0:T(8,128)(2,1)} async-done(((bf16[768,256]{1,0:T(8,128)(2,1)}), bf16[768,4096]{1,0:T(8,128)(2,1)}) %all-gather.3.cloned.1.call-update) | async-done | bytes 6291472 | tf_op jit(solution)/shard_map/all_gather | solution.py:75
  74.9 4.1 %fusion = f32[768]{0:T(1024)S(1)} fusion(bf16[768,4096]{1,0:T(8,128)(2,1)} %all-gather.3.cloned.1.call-done), kind=kLoop, calls=%fused_computation.4 | loop fusion | flops 9436416 | bytes 6294528 | tf_op jit(solution)/shard_map/reduce_sum | solution.py:17
  79.0 0.0 copy-start.1
  79.0 103.2 %all-gather.5.cloned.1.call-done = bf16[4096,1000]{0,1:T(8,128)(2,1)} async-done(((bf16[128,1000]{0,1:T(8,128)(2,1)}), bf16[4096,1000]{0,1:T(8,128)(2,1)}) %all-gather.5.cloned.1.call-update) | async-done | bytes 8192016 | tf_op jit(solution)/shard_map/all_gather | solution.py:78
  182.2 11.2 %fusion.15 = (f32[768]{0:T(1024)S(1)}, f32[768,1000]{0,1:T(8,128)S(1)}) fusion(bf16[4096,1000]{0,1:T(8,128)(2,1)} %all-gather.5.cloned.1.call-done, bf16[768,4096]{1,0:T(8,128)(2,1)} %all-gather.3.cloned.1.call-done, f32[4096]{0:T(1024)S(1)} %convert_element_type.10, f32[768]{0:T(1024)S(1)} %add_rsqrt_fusion), kind=kOutput, calls=%fused_computation.39 | convolution fusion | flops 6304805888 | bytes 17577984 | tf_op jit(solution)/shard_map/dot_general | solution.py:79
  193.4 0.0 copy-start
  193.4 0.0 copy-done.1
  193.4 1.4 fusion.7
  194.8 0.6 pad_maximum_fusion
  195.4 16.3 %shard_map.77 = f32[16,3072]{1,0:T(8,128)} custom-call(f32[1,3072]{1,0:T(1,128)} %bitcast.28), custom_call_target="tpu_custom_call" | custom-call | tf_op jit(solution)/shard_map/pallas_call | solution.py:61
  211.7 1.0 reshape.31
  212.7 0.2 fusion.14
  213.0 0.6 broadcast_in_dim.30.x_ref
  213.5 14.4 %shard_map.78 = f32[32,1536]{1,0:T(8,128)} custom-call(f32[1,1536]{1,0:T(1,128)} %broadcast_in_dim.30.x_ref), custom_call_target="tpu_custom_call" | custom-call | tf_op jit(solution)/shard_map/pallas_call | solution.py:61
  228.0 1.1 reshape.32
  229.1 0.2 fusion.13
  229.2 4.5 %gather_fusion.1 = f32[768]{0:T(1024)S(1)} fusion(f32[24576]{0:T(1024)S(1)} %bitcast.27, s32[1024]{0:T(1024)S(1)} %pad_clamp_fusion), kind=kCustom, calls=%fused_computation.1.clone | custom fusion | bytes 9216 | tf_op jit(solution)/shard_map/jit(_take)/gather | solution.py:101
  233.7 0.0 copy-done
  233.7 0.6 broadcast_select_fusion
  234.3 4.5 %gather_fusion = f32[768]{0:T(1024)S(1)} fusion(f32[24576]{0:T(1024)S(1)} %bitcast.26, s32[1024]{0:T(1024)S(1)} %pad_clamp_fusion), kind=kCustom, calls=%fused_computation.clone | custom fusion | bytes 9216 | tf_op jit(solution)/shard_map/jit(_take)/gather | solution.py:101
  238.8 0.6 broadcast_select_fusion.1
  (6 shorter events, 0.1 us)
Async XLA Ops:
  7.2 67.7 %all-gather.3.cloned.1.call-start = ((), (), s32[]{:S(2)}) async-start(), calls=%async_computation | async-start | bytes 6684672 | tf_op jit(solution)/shard_map/all_gather | solution.py:75
  7.9 174.3 %all-gather.5.cloned.1.call-start = ((), (), s32[]{:S(2)}) async-start(), calls=%async_computation.1 | async-start | bytes 8448000 | tf_op jit(solution)/shard_map/all_gather | solution.py:78
  79.0 114.4 %copy-start.1 = (s32[768]{0:T(1024)S(1)}, s32[768]{0:T(1024)}, u32[]{:S(2)}) copy-start(s32[768]{0:T(1024)} %param.9) | copy-start | bytes 9220
  193.4 40.3 %copy-start = (s32[768]{0:T(1024)S(1)}, s32[768]{0:T(1024)}, u32[]{:S(2)}) copy-start(s32[768]{0:T(1024)} %param.13) | copy-start | bytes 9220
Sparse Core Ops, SparseCore 0:
  10.0 64.8 all-gather.2
  78.0 104.2 all-gather.4

commit v2 on v1

--- a/solution.py
+++ b/solution.py
@@ -56,6 +56,71 @@
         incoming.wait_recv()
 
 
+def _rows_kernel(n_y, x_ref, o_ref, s1, r1, s2, r2):
+    me = lax.axis_index("voc")
+    g = lax.axis_index("grp")
+    width = x_ref.shape[1]
+    y = me // 2
+    c = me % 2
+    partner = y * 2 + 1 - c
+
+    def cols(v):
+        return pl.ds(pl.multiple_of(v * width, width), width)
+
+    def same_core(k):
+        return lax.rem(y + k, n_y) * 2 + c
+
+    def source(k):
+        return lax.rem(y + n_y - k, n_y) * 2 + c
+
+    barrier = pltpu.get_barrier_semaphore()
+    for k in range(1, n_y):
+        pl.semaphore_signal(barrier, inc=1, device_id=(g, same_core(k)), device_id_type=MESH)
+    pl.semaphore_signal(barrier, inc=1, device_id=(g, partner), device_id_type=MESH)
+    pl.semaphore_wait(barrier, n_y)
+
+    def remote(src, dst, send, recv, target):
+        return pltpu.make_async_remote_copy(
+            src_ref=src, dst_ref=dst, send_sem=send, recv_sem=recv,
+            device_id=(g, target), device_id_type=MESH,
+        )
+
+    sends = []
+    for k in range(1, n_y):
+        copy = remote(x_ref, o_ref.at[:, cols(me)], s1.at[k], r1.at[k], same_core(k))
+        copy.start()
+        sends.append(copy)
+    copy = remote(x_ref, o_ref.at[:, cols(me)], s2.at[0], r2.at[0], partner)
+    copy.start()
+    sends.append(copy)
+    o_ref[:, cols(me)] = x_ref[...]
+    for k in range(1, n_y):
+        block = o_ref.at[:, cols(source(k))]
+        remote(x_ref, block, s1.at[k], r1.at[k], source(k)).wait_recv()
+        copy = remote(block, block, s2.at[k], r2.at[k], partner)
+        copy.start()
+        sends.append(copy)
+    for k in range(n_y):
+        other = lax.rem(y + n_y - k, n_y) * 2 + 1 - c
+        block = o_ref.at[:, cols(other)]
+        remote(block, block, s2.at[k], r2.at[k], partner).wait_recv()
+    for copy in sends:
+        copy.wait_send()
+
+
+def gather_rows(hidden, n_voc):
+    rows, width = hidden.shape
+    n_y = n_voc // 2
+    return pl.pallas_call(
+        functools.partial(_rows_kernel, n_y),
+        out_shape=jax.ShapeDtypeStruct((rows, width * n_voc), hidden.dtype),
+        in_specs=[pl.BlockSpec(memory_space=pltpu.VMEM)],
+        out_specs=pl.BlockSpec(memory_space=pltpu.VMEM),
+        scratch_shapes=[pltpu.SemaphoreType.DMA((n_y,))] * 4,
+        compiler_params=pltpu.CompilerParams(collective_id=2, has_side_effects=True),
+    )(hidden)
+
+
 def share(row, axis, other, n, collective_id):
     width = row.shape[1]
     return pl.pallas_call(
@@ -72,7 +137,7 @@
     tok_rows = hidden.shape[0]
     positions = jnp.arange(tok_rows, dtype=jnp.int32)
     live_rows = positions < row_count[0]
-    full_rows = lax.all_gather(hidden, "voc", axis=1, tiled=True)
+    full_rows = gather_rows(hidden, n_voc)
     normed = normalize(full_rows, norm_gain)
     vocab_local = head_weight.shape[1]
     piece = lax.all_gather(head_weight, "grp", axis=0, tiled=True)

time: 247 us -> 187 us (0.76)
  waiting for transfers between devices: 169 us -> 28.7 us
  Pallas kernels: 30.7 us -> 112 us
    pallas_call x0 -> x1, Pallas kernels: none -> 81.8 us  [gather_rows(): pl.pallas_call(functools.partial(_rows_kernel, n_y), out_shape=jax.ShapeD...]
    all_gather x1, waiting for transfers between devices: 103 us -> 28 us  [local(): piece = lax.all_gather(head_weight, 'grp', axis=0, tiled=True)]
    all_gather x1 -> x0, waiting for transfers between devices: 64.2 us -> none  [local(): full_rows = lax.all_gather(hidden, 'voc', axis=1, tiled=True)]
  transfers between devices with their start and end apart: 2 -> 1, of which waited for: 2 -> 1; matrix products, arithmetic and copies ran while one was open for 2% -> 2% of each run, Pallas kernels for 0% -> 44%
where the time goes in v2:
time: 187 us
  Pallas kernels  112 us (60%)
  waiting for transfers between devices  28.7 us (15%)
  between operations  14.9 us (8%)
  local copies, waits for them, and re-layouts  11.7 us (6%)
  matrix products  11.2 us (6%)
  other arithmetic  7.68 us (4%)
    pallas_call x1, Pallas kernels, gather_rows(): pl.pallas_call(functools.partial(_rows_kernel, n_y), out_shape=jax.ShapeD...  81.8 us
    pallas_call x2, Pallas kernels, share(): pl.pallas_call(functools.partial(_share_kernel, axis, other, n), out_shap...  30.7 us
    all_gather x1, waiting for transfers between devices, local(): piece = lax.all_gather(head_weight, 'grp', axis=0, tiled=True)  28 us
    dot_general x1, matrix products, local(): logits = jnp.dot(normed, piece, preferred_element_type=jnp.float32)  11.2 us
    gather x1, local copies, waits for them, and re-layouts, local(): jnp.take(every_entropy, return_from, axis=0)  4.46 us
    gather x1, local copies, waits for them, and re-layouts, local(): jnp.take(every_logp, return_from, axis=0)  4.45 us
    reduce_sum x1, other arithmetic, normalize(): jnp.mean(values * values, axis=1, keepdims=True) + EPSILON  4.27 us
  transfers between devices with their start and end apart: 1, of which 1 were waited for; matrix products, arithmetic and copies ran while one was open for 2% of the time, Pallas kernels for 44%

profile of v2, /device:TPU:1, one launch (start us, length us, event | category | flops | bytes accessed | tf_op | source)
XLA Modules:
  0.0 186.7 jit_solution(4293410737018057822)
XLA Ops:
  7.2 0.0 copy-start.1
  7.2 0.0 copy-start
  7.2 0.0 all-gather.2.cloned.1.call-start
  7.2 0.7 all-gather.2.cloned.1.call-update
  7.9 81.8 %shard_map.77 = bf16[768,4096]{1,0:T(8,128)(2,1)} custom-call(bf16[768,256]{1,0:T(8,128)(2,1)} %x_ref.1), custom_call_target="tpu_custom_call" | custom-call | tf_op jit(solution)/shard_map/pallas_call | solution.py:114
  89.7 0.0 copy-done.1
  90.4 0.0 copy-done
  90.5 4.3 %fusion = f32[768]{0:T(1024)S(1)} fusion(bf16[768,4096]{1,0:T(8,128)(2,1)} %shard_map.77), kind=kLoop, calls=%fused_computation.4 | loop fusion | flops 9436416 | bytes 6294528 | tf_op jit(solution)/shard_map/reduce_sum | solution.py:17
  94.7 0.0 copy-start.2
  94.8 28.0 %all-gather.2.cloned.1.call-done = bf16[4096,1000]{0,1:T(8,128)(2,1)} async-done(((bf16[128,1000]{0,1:T(8,128)(2,1)}), bf16[4096,1000]{0,1:T(8,128)(2,1)}) %all-gather.2.cloned.1.call-update) | async-done | bytes 8192016 | tf_op jit(solution)/shard_map/all_gather | solution.py:143
  122.7 11.2 %fusion.15 = (f32[768]{0:T(1024)S(1)}, f32[768,1000]{0,1:T(8,128)S(1)}) fusion(bf16[4096,1000]{0,1:T(8,128)(2,1)} %all-gather.2.cloned.1.call-done, bf16[768,4096]{1,0:T(8,128)(2,1)} %shard_map.77, f32[4096]{0:T(1024)S(1)} %convert_element_type.10, f32[768]{0:T(1024)S(1)} %add_rsqrt_fusion), kind=kOutput, calls=%fused_computation.39 | convolution fusion | flops 6304805888 | bytes 17577984 | tf_op jit(solution)/shard_map/dot_general | solution.py:144
  133.9 0.0 copy-done.2
  133.9 1.4 fusion.7
  135.3 0.6 pad_maximum_fusion
  135.9 16.3 %shard_map.78 = f32[16,3072]{1,0:T(8,128)} custom-call(f32[1,3072]{1,0:T(1,128)} %bitcast.28), custom_call_target="tpu_custom_call" | custom-call | tf_op jit(solution)/shard_map/pallas_call | solution.py:126
  152.2 1.0 reshape.31
  153.2 0.2 fusion.14
  153.5 0.6 broadcast_in_dim.30.x_ref
  154.1 14.4 %shard_map.79 = f32[32,1536]{1,0:T(8,128)} custom-call(f32[1,1536]{1,0:T(1,128)} %broadcast_in_dim.30.x_ref), custom_call_target="tpu_custom_call" | custom-call | tf_op jit(solution)/shard_map/pallas_call | solution.py:126
  168.5 1.1 reshape.32
  169.5 0.2 fusion.13
  169.7 4.5 %gather_fusion.1 = f32[768]{0:T(1024)S(1)} fusion(f32[24576]{0:T(1024)S(1)} %bitcast.27, s32[1024]{0:T(1024)S(1)} %pad_clamp_fusion), kind=kCustom, calls=%fused_computation.1.clone | custom fusion | bytes 9216 | tf_op jit(solution)/shard_map/jit(_take)/gather | solution.py:166
  174.2 0.6 broadcast_select_fusion
  174.8 4.5 %gather_fusion = f32[768]{0:T(1024)S(1)} fusion(f32[24576]{0:T(1024)S(1)} %bitcast.26, s32[1024]{0:T(1024)S(1)} %pad_clamp_fusion), kind=kCustom, calls=%fused_computation.clone | custom fusion | bytes 9216 | tf_op jit(solution)/shard_map/jit(_take)/gather | solution.py:166
  179.2 0.6 broadcast_select_fusion.1
  (8 shorter events, 0.1 us)
Async XLA Ops:
  7.2 82.6 %copy-start.1 = (bf16[4096]{0:T(1024)(128)(2,1)S(1)}, bf16[4096]{0:T(1024)(128)(2,1)}, u32[]{:S(2)}) copy-start(bf16[4096]{0:T(1024)(128)(2,1)} %param.11) | copy-start | bytes 24580
  7.2 83.3 %copy-start = (s32[768]{0:T(1024)S(1)}, s32[768]{0:T(1024)}, u32[]{:S(2)}) copy-start(s32[768]{0:T(1024)} %param.13) | copy-start | bytes 9220
  7.2 115.5 %all-gather.2.cloned.1.call-start = ((), (), s32[]{:S(2)}) async-start(), calls=%async_computation | async-start | bytes 8448000 | tf_op jit(solution)/shard_map/all_gather | solution.py:143
  94.7 39.2 %copy-start.2 = (s32[768]{0:T(1024)S(1)}, s32[768]{0:T(1024)}, u32[]{:S(2)}) copy-start(s32[768]{0:T(1024)} %param.9) | copy-start | bytes 9220
Sparse Core Ops, SparseCore 0:
  11.1 111.6 all-gather.1

commit v3 on v2

--- a/solution.py
+++ b/solution.py
@@ -121,6 +121,109 @@
     )(hidden)
 
 
+class _Ring:
+    def __init__(self, pos, n, device, slot, own, sems):
+        self.pos, self.n, self.device, self.slot, self.own = pos, n, device, slot, own
+        self.sems = sems
+        self.right = n // 2
+        self.left = n - 1 - self.right
+        self.copies = []
+
+    def _copy(self, origin, kind, s, target):
+        view = self.slot(origin)
+        return pltpu.make_async_remote_copy(
+            src_ref=view, dst_ref=view,
+            send_sem=self.sems.at[kind, s], recv_sem=self.sems.at[kind + 1, s],
+            device_id=self.device(target), device_id_type=MESH,
+        )
+
+    def _origin(self, step, sign):
+        return lax.rem(self.pos + sign * step + 2 * self.n, self.n)
+
+    def step(self, s):
+        for count, kind, sign in ((self.right, 0, 1), (self.left, 2, -1)):
+            if s > count:
+                continue
+            target = self._origin(1, sign)
+            origin = self._origin(s - 1, -sign)
+            if s == 1:
+                src = self.own
+            else:
+                self._copy(origin, kind, s - 2, target).wait_recv()
+                src = self.slot(origin)
+            copy = pltpu.make_async_remote_copy(
+                src_ref=src, dst_ref=self.slot(origin),
+                send_sem=self.sems.at[kind, s - 1], recv_sem=self.sems.at[kind + 1, s - 1],
+                device_id=self.device(target), device_id_type=MESH,
+            )
+            copy.start()
+            self.copies.append(copy)
+
+    def finish_recv(self):
+        for count, kind, sign in ((self.right, 0, 1), (self.left, 2, -1)):
+            if count:
+                self._copy(self._origin(count, -sign), kind, count - 1, self._origin(1, sign)).wait_recv()
+
+    def finish_send(self):
+        for copy in self.copies:
+            copy.wait_send()
+
+
+def _head_kernel(n_x, n_z, x_ref, o_ref, local_sem, sems):
+    me = lax.axis_index("grp")
+    v = lax.axis_index("voc")
+    x = me // n_z
+    z = me % n_z
+    half = x_ref.shape[0] // 2
+    lo, hi = pl.ds(0, half), pl.ds(half, half)
+
+    def along_x(t):
+        return (t * n_z + z, v)
+
+    def along_z(t):
+        return (x * n_z + t, v)
+
+    barrier = pltpu.get_barrier_semaphore()
+    neighbours = [along_x(lax.rem(x + 1, n_x)), along_x(lax.rem(x + n_x - 1, n_x)),
+                  along_z(lax.rem(z + 1, n_z)), along_z(lax.rem(z + n_z - 1, n_z))]
+    for target in neighbours:
+        pl.semaphore_signal(barrier, inc=1, device_id=target, device_id_type=MESH)
+    pl.semaphore_wait(barrier, len(neighbours))
+
+    own = pltpu.make_async_copy(x_ref, o_ref.at[x, z], local_sem.at[0])
+    own.start()
+    first_x = _Ring(x, n_x, along_x, lambda t: o_ref.at[t, z, lo], x_ref.at[lo], sems.at[0])
+    first_z = _Ring(z, n_z, along_z, lambda t: o_ref.at[x, t, hi], x_ref.at[hi], sems.at[1])
+    for s in range(1, max(n_x, n_z)):
+        first_x.step(s)
+        first_z.step(s)
+    own.wait()
+    first_x.finish_recv()
+    first_z.finish_recv()
+    second_z = _Ring(z, n_z, along_z, lambda t: o_ref.at[:, t, lo], o_ref.at[:, z, lo], sems.at[2])
+    second_x = _Ring(x, n_x, along_x, lambda t: o_ref.at[t, :, hi], o_ref.at[x, :, hi], sems.at[3])
+    for s in range(1, max(n_x, n_z)):
+        second_z.step(s)
+        second_x.step(s)
+    second_z.finish_recv()
+    second_x.finish_recv()
+    for ring in (first_x, first_z, second_z, second_x):
+        ring.finish_send()
+
+
+def gather_head(piece, n_x, n_z):
+    rows, width = piece.shape
+    full = pl.pallas_call(
+        functools.partial(_head_kernel, n_x, n_z),
+        out_shape=jax.ShapeDtypeStruct((n_x, n_z, rows, width), piece.dtype),
+        in_specs=[pl.BlockSpec(memory_space=pltpu.VMEM)],
+        out_specs=pl.BlockSpec(memory_space=pltpu.VMEM),
+        scratch_shapes=[pltpu.SemaphoreType.DMA((1,)), pltpu.SemaphoreType.DMA((4, 4, max(n_x, n_z)))],
+        compiler_params=pltpu.CompilerParams(collective_id=3, has_side_effects=True),
+    )(piece)
+    return full.reshape(n_x * n_z * rows, width)
+
+
 def share(row, axis, other, n, collective_id):
     width = row.shape[1]
     return pl.pallas_call(
@@ -133,14 +236,14 @@
     )(row)
 
 
-def local(hidden, targets, row_count, norm_gain, head_weight, return_from, *, n_voc, n_grp):
+def local(hidden, targets, row_count, norm_gain, head_weight, return_from, *, n_voc, n_grp, n_x, n_z):
     tok_rows = hidden.shape[0]
     positions = jnp.arange(tok_rows, dtype=jnp.int32)
     live_rows = positions < row_count[0]
-    full_rows = gather_rows(hidden, n_voc)
+    full_rows = lax.all_gather(hidden, "voc", axis=1, tiled=True)
     normed = normalize(full_rows, norm_gain)
     vocab_local = head_weight.shape[1]
-    piece = lax.all_gather(head_weight, "grp", axis=0, tiled=True)
+    piece = gather_head(head_weight, n_x, n_z)
     logits = jnp.dot(normed, piece, preferred_element_type=jnp.float32)
     peak = jnp.max(logits, axis=1)
     shifted = jnp.exp(logits - peak[:, None])
@@ -168,7 +271,9 @@
 
 def solution(mesh):
     placed = (P("grp", "voc"), P("grp"), P("grp"), P(), P("grp", "voc"), P("grp"))
-    body = functools.partial(local, n_voc=mesh.shape["voc"], n_grp=mesh.shape["grp"])
+    n_grp = mesh.shape["grp"]
+    n_z = len({device.coords[2] for device in mesh.devices[:, 0]})
+    body = functools.partial(local, n_voc=mesh.shape["voc"], n_grp=n_grp, n_x=n_grp // n_z, n_z=n_z)
     return jax.shard_map(
         body, mesh=mesh, in_specs=placed, out_specs=(P("grp"), P("grp")), check_vma=False
     )

time: 187 us -> 158 us (0.84)
  waiting for transfers between devices: 28.7 us -> 0.7 us
  local copies, waits for them, and re-layouts: 11.7 us -> 13.9 us
  Pallas kernels: 112 us -> 110 us
    all_gather x1, waiting for transfers between devices: 28 us -> 0.02 us  [local(): full_rows = lax.all_gather(hidden, 'voc', axis=1, tiled=True)]
    pallas_call x1, Pallas kernels: 81.8 us -> 75.3 us  [gather_head(): pl.pallas_call(functools.partial(_head_kernel, n_x, n_z), out_shape=jax.S...]
    pallas_call x2, Pallas kernels: 30.7 us -> 35 us  [share(): pl.pallas_call(functools.partial(_share_kernel, axis, other, n), out_shap...]
    unnamed x6 -> x9, local copies, waits for them, and re-layouts: 0.01 us -> 2.19 us
  transfers between devices with their start and end apart: 1 -> 1, of which waited for: 1 -> 0; matrix products, arithmetic and copies ran while one was open for 2% -> 1% of each run, Pallas kernels for 44% -> 48%
where the time goes in v3:
time: 158 us
  Pallas kernels  110 us (70%)
  between operations  14.9 us (9%)
  local copies, waits for them, and re-layouts  13.9 us (9%)
  matrix products  10.3 us (7%)
  other arithmetic  7.64 us (5%)
    pallas_call x1, Pallas kernels, gather_head(): pl.pallas_call(functools.partial(_head_kernel, n_x, n_z), out_shape=jax.S...  75.3 us
    pallas_call x2, Pallas kernels, share(): pl.pallas_call(functools.partial(_share_kernel, axis, other, n), out_shap...  35 us
    dot_general x1, matrix products, local(): logits = jnp.dot(normed, piece, preferred_element_type=jnp.float32)  10.3 us
    gather x1, local copies, waits for them, and re-layouts, local(): jnp.take(every_entropy, return_from, axis=0)  4.46 us
    gather x1, local copies, waits for them, and re-layouts, local(): jnp.take(every_logp, return_from, axis=0)  4.45 us
    reduce_sum x1, other arithmetic, normalize(): jnp.mean(values * values, axis=1, keepdims=True) + EPSILON  4.22 us
  transfers between devices with their start and end apart: 1, of which 0 were waited for; matrix products, arithmetic and copies ran while one was open for 1% of the time, Pallas kernels for 48%

profile of v3, /device:TPU:1, one launch (start us, length us, event | category | flops | bytes accessed | tf_op | source)
XLA Modules:
  0.0 157.8 jit_solution(6240440489323662656)
XLA Ops:
  7.2 0.0 copy-start.2
  7.2 0.0 copy-start.1
  7.2 0.0 all-gather.2.cloned.1.call-start
  7.2 0.7 all-gather.2.cloned.1.call-update
  7.9 1.8 %copy.11.x_ref = bf16[128,1000]{1,0:T(8,128)(2,1)} copy(bf16[128,1000]{0,1:T(8,128)(2,1)} %param.12) | data formatting | bytes 512000 | tf_op args[4]
  9.7 75.3 %shard_map.77 = bf16[4,8,128,1000]{3,2,1,0:T(8,128)(2,1)} custom-call(bf16[128,1000]{1,0:T(8,128)(2,1)} %copy.11.x_ref), custom_call_target="tpu_custom_call" | custom-call | tf_op jit(solution)/shard_map/pallas_call | solution.py:216
  85.1 0.0 copy-done.2
  85.8 0.0 copy-done.1
  85.8 0.0 all-gather.2.cloned.1.call-done
  85.9 0.0 copy-start
  85.9 4.2 %fusion = f32[768]{0:T(1024)S(1)} fusion(bf16[768,4096]{1,0:T(8,128)(2,1)} %all-gather.2.cloned.1.call-done), kind=kLoop, calls=%fused_computation.4 | loop fusion | flops 9436416 | bytes 6294528 | tf_op jit(solution)/shard_map/reduce_sum | solution.py:17
  90.1 0.4 copy-done
  90.5 0.0 copy-start.3
  90.5 10.3 %fusion.15 = (f32[768]{0:T(1024)S(1)}, f32[768,1000]{0,1:T(8,128)S(1)}) fusion(bf16[4096,1000]{1,0:T(8,128)(2,1)} %bitcast.29, bf16[768,4096]{1,0:T(8,128)(2,1)S(1)} %copy-done, f32[4096]{0:T(1024)S(1)} %convert_element_type.10, f32[768]{0:T(1024)S(1)} %add_rsqrt_fusion), kind=kOutput, calls=%fused_computation.39 | convolution fusion | flops 6304805888 | bytes 17577984 | tf_op jit(solution)/shard_map/dot_general | solution.py:247
  100.7 0.0 copy-done.3
  100.7 1.4 fusion.7
  102.1 0.6 pad_maximum_fusion
  102.7 19.4 %shard_map.78 = f32[16,3072]{1,0:T(8,128)} custom-call(f32[1,3072]{1,0:T(1,128)} %bitcast.30), custom_call_target="tpu_custom_call" | custom-call | tf_op jit(solution)/shard_map/pallas_call | solution.py:229
  122.2 1.0 reshape.35
  123.2 0.2 fusion.14
  123.4 0.6 broadcast_in_dim.30.x_ref
  124.0 15.6 %shard_map.79 = f32[32,1536]{1,0:T(8,128)} custom-call(f32[1,1536]{1,0:T(1,128)} %broadcast_in_dim.30.x_ref), custom_call_target="tpu_custom_call" | custom-call | tf_op jit(solution)/shard_map/pallas_call | solution.py:229
  139.6 1.1 reshape.36
  140.7 0.2 fusion.13
  140.8 4.5 %gather_fusion.1 = f32[768]{0:T(1024)S(1)} fusion(f32[24576]{0:T(1024)S(1)} %bitcast.28, s32[1024]{0:T(1024)S(1)} %pad_clamp_fusion), kind=kCustom, calls=%fused_computation.1.clone | custom fusion | bytes 9216 | tf_op jit(solution)/shard_map/jit(_take)/gather | solution.py:269
  145.3 0.6 broadcast_select_fusion
  145.9 4.5 %gather_fusion = f32[768]{0:T(1024)S(1)} fusion(f32[24576]{0:T(1024)S(1)} %bitcast.27, s32[1024]{0:T(1024)S(1)} %pad_clamp_fusion), kind=kCustom, calls=%fused_computation.clone | custom fusion | bytes 9216 | tf_op jit(solution)/shard_map/jit(_take)/gather | solution.py:269
  150.4 0.6 broadcast_select_fusion.1
  (8 shorter events, 0.1 us)
Async XLA Ops:
  7.2 77.9 %copy-start.2 = (bf16[4096]{0:T(1024)(128)(2,1)S(1)}, bf16[4096]{0:T(1024)(128)(2,1)}, u32[]{:S(2)}) copy-start(bf16[4096]{0:T(1024)(128)(2,1)} %param.11) | copy-start | bytes 24580
  7.2 78.6 %copy-start.1 = (s32[768]{0:T(1024)S(1)}, s32[768]{0:T(1024)}, u32[]{:S(2)}) copy-start(s32[768]{0:T(1024)} %param.13) | copy-start | bytes 9220
  7.2 78.7 %all-gather.2.cloned.1.call-start = ((), (), s32[]{:S(2)}) async-start(), calls=%async_computation | async-start | bytes 6684672 | tf_op jit(solution)/shard_map/all_gather | solution.py:243
  85.9 4.6 %copy-start = (bf16[768,4096]{1,0:T(8,128)(2,1)S(1)}, bf16[768,4096]{1,0:T(8,128)(2,1)}, u32[]{:S(2)}) copy-start(bf16[768,4096]{1,0:T(8,128)(2,1)} %all-gather.2.cloned.1.call-done) | copy-start | bytes 18874372
  90.5 10.3 %copy-start.3 = (s32[768]{0:T(1024)S(1)}, s32[768]{0:T(1024)}, u32[]{:S(2)}) copy-start(s32[768]{0:T(1024)} %param.9) | copy-start | bytes 9220
Sparse Core Ops, SparseCore 0:
  10.1 64.3 all-gather.1

commit v4 on v1

--- a/solution.py
+++ b/solution.py
@@ -56,6 +56,165 @@
         incoming.wait_recv()
 
 
+class _Ring:
+    def __init__(self, pos, n, device, slot, own, sems, on_arrival=None):
+        self.pos, self.n, self.device, self.slot, self.own = pos, n, device, slot, own
+        self.sems = sems
+        self.on_arrival = on_arrival
+        self.right = n // 2
+        self.left = n - 1 - self.right
+        self.copies = []
+
+    def _copy(self, origin, kind, s, target):
+        view = self.slot(origin)
+        return pltpu.make_async_remote_copy(
+            src_ref=view, dst_ref=view,
+            send_sem=self.sems.at[kind, s], recv_sem=self.sems.at[kind + 1, s],
+            device_id=self.device(target), device_id_type=MESH,
+        )
+
+    def _origin(self, step, sign):
+        return lax.rem(self.pos + sign * step + 2 * self.n, self.n)
+
+    def step(self, s):
+        for count, kind, sign in ((self.right, 0, 1), (self.left, 2, -1)):
+            if s > count:
+                continue
+            target = self._origin(1, sign)
+            origin = self._origin(s - 1, -sign)
+            if s == 1:
+                src = self.own
+            else:
+                self._copy(origin, kind, s - 2, target).wait_recv()
+                if self.on_arrival is not None:
+                    self.on_arrival(origin)
+                src = self.slot(origin)
+            copy = pltpu.make_async_remote_copy(
+                src_ref=src, dst_ref=self.slot(origin),
+                send_sem=self.sems.at[kind, s - 1], recv_sem=self.sems.at[kind + 1, s - 1],
+                device_id=self.device(target), device_id_type=MESH,
+            )
+            copy.start()
+            self.copies.append(copy)
+
+    def finish_recv(self):
+        for count, kind, sign in ((self.right, 0, 1), (self.left, 2, -1)):
+            if count:
+                origin = self._origin(count, -sign)
+                self._copy(origin, kind, count - 1, self._origin(1, sign)).wait_recv()
+                if self.on_arrival is not None:
+                    self.on_arrival(origin)
+
+    def finish_send(self):
+        for copy in self.copies:
+            copy.wait_send()
+
+
+def _gather_kernel(n_x, n_z, n_y, rows_ref, head_ref, rows_out, head_out, local_sem, sems, pair_sems):
+    me = lax.axis_index("grp")
+    v = lax.axis_index("voc")
+    x = me // n_z
+    z = me % n_z
+    y = v // 2
+    c = v % 2
+    partner = y * 2 + 1 - c
+    half = head_ref.shape[0] // 2
+    lo, hi = pl.ds(0, half), pl.ds(half, half)
+    width = rows_ref.shape[1]
+
+    def cols(t):
+        return pl.ds(pl.multiple_of(t * width, width), width)
+
+    def along_x(t):
+        return (t * n_z + z, v)
+
+    def along_z(t):
+        return (x * n_z + t, v)
+
+    def along_y(t):
+        return (me, t * 2 + c)
+
+    barrier = pltpu.get_barrier_semaphore()
+    neighbours = [along_x(lax.rem(x + 1, n_x)), along_x(lax.rem(x + n_x - 1, n_x)),
+                  along_z(lax.rem(z + 1, n_z)), along_z(lax.rem(z + n_z - 1, n_z)),
+                  along_y(lax.rem(y + 1, n_y)), along_y(lax.rem(y + n_y - 1, n_y)),
+                  (me, partner)]
+    for target in neighbours:
+        pl.semaphore_signal(barrier, inc=1, device_id=target, device_id_type=MESH)
+    pl.semaphore_wait(barrier, len(neighbours))
+
+    def to_partner(src, t):
+        return pltpu.make_async_remote_copy(
+            src_ref=src, dst_ref=rows_out.at[:, cols(t * 2 + c)],
+            send_sem=pair_sems.at[0, t], recv_sem=pair_sems.at[1, t],
+            device_id=(me, partner), device_id_type=MESH,
+        )
+
+    pair_copies = []
+
+    def forward(t):
+        copy = to_partner(rows_out.at[:, cols(t * 2 + c)], t)
+        copy.start()
+        pair_copies.append(copy)
+
+    own = pltpu.make_async_copy(head_ref, head_out.at[x, z], local_sem.at[0])
+    own.start()
+    copy = to_partner(rows_ref, y)
+    copy.start()
+    pair_copies.append(copy)
+    rows_out[:, cols(v)] = rows_ref[...]
+    rows = _Ring(y, n_y, along_y, lambda t: rows_out.at[:, cols(t * 2 + c)], rows_ref, sems.at[4], forward)
+    first_x = _Ring(x, n_x, along_x, lambda t: head_out.at[t, z, lo], head_ref.at[lo], sems.at[0])
+    first_z = _Ring(z, n_z, along_z, lambda t: head_out.at[x, t, hi], head_ref.at[hi], sems.at[1])
+    steps = max(n_x, n_z, n_y)
+    rows.step(1)
+    for s in range(1, steps):
+        first_x.step(s)
+        first_z.step(s)
+    own.wait()
+    first_x.finish_recv()
+    first_z.finish_recv()
+    second_z = _Ring(z, n_z, along_z, lambda t: head_out.at[:, t, lo], head_out.at[:, z, lo], sems.at[2])
+    second_x = _Ring(x, n_x, along_x, lambda t: head_out.at[t, :, hi], head_out.at[x, :, hi], sems.at[3])
+    for s in range(1, steps):
+        second_z.step(s)
+        second_x.step(s)
+        rows.step(s + 1)
+    rows.finish_recv()
+    second_z.finish_recv()
+    second_x.finish_recv()
+    for t in range(n_y):
+        other = t * 2 + 1 - c
+        block = rows_out.at[:, cols(other)]
+        pltpu.make_async_remote_copy(
+            src_ref=block, dst_ref=block,
+            send_sem=pair_sems.at[0, t], recv_sem=pair_sems.at[1, t],
+            device_id=(me, partner), device_id_type=MESH,
+        ).wait_recv()
+    for ring in (first_x, first_z, second_z, second_x, rows):
+        ring.finish_send()
+    for copy in pair_copies:
+        copy.wait_send()
+
+
+def gather_both(hidden, piece, n_x, n_z, n_voc):
+    rows, width = hidden.shape
+    depth, vocab = piece.shape
+    n_y = n_voc // 2
+    steps = max(n_x, n_z, n_y)
+    full_rows, full_head = pl.pallas_call(
+        functools.partial(_gather_kernel, n_x, n_z, n_y),
+        out_shape=(jax.ShapeDtypeStruct((rows, width * n_voc), hidden.dtype),
+                   jax.ShapeDtypeStruct((n_x, n_z, depth, vocab), piece.dtype)),
+        in_specs=[pl.BlockSpec(memory_space=pltpu.VMEM)] * 2,
+        out_specs=(pl.BlockSpec(memory_space=pltpu.VMEM), pl.BlockSpec(memory_space=pltpu.VMEM)),
+        scratch_shapes=[pltpu.SemaphoreType.DMA((1,)), pltpu.SemaphoreType.DMA((5, 4, steps)),
+                        pltpu.SemaphoreType.DMA((2, n_y))],
+        compiler_params=pltpu.CompilerParams(collective_id=3, has_side_effects=True),
+    )(hidden, piece)
+    return full_rows, full_head.reshape(n_x * n_z * depth, vocab)
+
+
 def share(row, axis, other, n, collective_id):
     width = row.shape[1]
     return pl.pallas_call(
@@ -68,14 +227,13 @@
     )(row)
 
 
-def local(hidden, targets, row_count, norm_gain, head_weight, return_from, *, n_voc, n_grp):
+def local(hidden, targets, row_count, norm_gain, head_weight, return_from, *, n_voc, n_grp, n_x, n_z):
     tok_rows = hidden.shape[0]
     positions = jnp.arange(tok_rows, dtype=jnp.int32)
     live_rows = positions < row_count[0]
-    full_rows = lax.all_gather(hidden, "voc", axis=1, tiled=True)
+    full_rows, piece = gather_both(hidden, head_weight, n_x, n_z, n_voc)
     normed = normalize(full_rows, norm_gain)
     vocab_local = head_weight.shape[1]
-    piece = lax.all_gather(head_weight, "grp", axis=0, tiled=True)
     logits = jnp.dot(normed, piece, preferred_element_type=jnp.float32)
     peak = jnp.max(logits, axis=1)
     shifted = jnp.exp(logits - peak[:, None])
@@ -103,7 +261,9 @@
 
 def solution(mesh):
     placed = (P("grp", "voc"), P("grp"), P("grp"), P(), P("grp", "voc"), P("grp"))
-    body = functools.partial(local, n_voc=mesh.shape["voc"], n_grp=mesh.shape["grp"])
+    n_grp = mesh.shape["grp"]
+    n_z = len({device.coords[2] for device in mesh.devices[:, 0]})
+    body = functools.partial(local, n_voc=mesh.shape["voc"], n_grp=n_grp, n_x=n_grp // n_z, n_z=n_z)
     return jax.shard_map(
         body, mesh=mesh, in_specs=placed, out_specs=(P("grp"), P("grp")), check_vma=False
     )

time: 247 us -> 146 us (0.59)
  waiting for transfers between devices: 169 us -> 0 us
  Pallas kernels: 30.7 us -> 112 us
  between operations: 14.8 us -> 1.47 us
    all_gather x2 -> x0, waiting for transfers between devices: 167 us -> none  [the longest x1 103 us: local(): piece = lax.all_gather(head_weight, 'grp', axis=0, tiled=True)]
    pallas_call x0 -> x1, Pallas kernels: none -> 80.9 us  [gather_both(): pl.pallas_call(functools.partial(_gather_kernel, n_x, n_z, n_y), out_shap...]
  transfers between devices with their start and end apart: 2 -> 0, of which waited for: 2 -> 0; matrix products, arithmetic and copies ran while one was open for 2% -> 0% of each run, Pallas kernels for 0% -> 0%
where the time goes in v4:
time: 146 us; the launch traced here: 145 us
  Pallas kernels  112 us (77%)
  local copies, waits for them, and re-layouts  13.9 us (10%)
  matrix products  10.3 us (7%)
  other arithmetic  7.64 us (5%)
  between operations  1.47 us (1%)
    pallas_call x1, Pallas kernels, gather_both(): pl.pallas_call(functools.partial(_gather_kernel, n_x, n_z, n_y), out_shap...  80.9 us
    pallas_call x2, Pallas kernels, share(): pl.pallas_call(functools.partial(_share_kernel, axis, other, n), out_shap...  31.3 us
    dot_general x1, matrix products, local(): logits = jnp.dot(normed, piece, preferred_element_type=jnp.float32)  10.3 us
    gather x1, local copies, waits for them, and re-layouts, local(): jnp.take(every_entropy, return_from, axis=0)  4.46 us
    gather x1, local copies, waits for them, and re-layouts, local(): jnp.take(every_logp, return_from, axis=0)  4.45 us
    reduce_sum x1, other arithmetic, normalize(): jnp.mean(values * values, axis=1, keepdims=True) + EPSILON  4.22 us

profile of v4, /device:TPU:1, one launch (start us, length us, event | category | flops | bytes accessed | tf_op | source)
XLA Modules:
  0.0 145.5 jit_solution(11717286230946821666)
XLA Ops:
  0.6 0.0 copy-start.2
  0.6 1.8 %copy.11.head_ref = bf16[128,1000]{1,0:T(8,128)(2,1)} copy(bf16[128,1000]{0,1:T(8,128)(2,1)} %param.12) | data formatting | bytes 512000 | tf_op args[4]
  2.5 80.9 %shard_map.77 = (bf16[768,4096]{1,0:T(8,128)(2,1)}, bf16[4,8,128,1000]{3,2,1,0:T(8,128)(2,1)}) custom-call(bf16[768,256]{1,0:T(8,128)(2,1)} %rows_ref.1, bf16[128,1000]{1,0:T(8,128)(2,1)} %copy.11.head_ref), custom_call_target="tpu_custom_call" | custom-call | tf_op jit(solution)/shard_map/pallas_call | solution.py:205
  83.3 0.0 copy-start
  83.4 4.2 %fusion = f32[768]{0:T(1024)S(1)} fusion(bf16[768,4096]{1,0:T(8,128)(2,1)} %get-tuple-element.5), kind=kLoop, calls=%fused_computation.4 | loop fusion | flops 9436416 | bytes 6294528 | tf_op jit(solution)/shard_map/reduce_sum | solution.py:17
  87.6 0.0 copy-done.2
  87.6 0.3 copy-done
  87.9 0.0 copy-start.3
  88.0 0.0 copy-start.1
  88.0 10.3 %fusion.15 = (f32[768]{0:T(1024)S(1)}, f32[768,1000]{0,1:T(8,128)S(1)}) fusion(bf16[4096,1000]{1,0:T(8,128)(2,1)} %bitcast.30, bf16[768,4096]{1,0:T(8,128)(2,1)S(1)} %copy-done, f32[4096]{0:T(1024)S(1)} %convert_element_type.10, f32[768]{0:T(1024)S(1)} %add_rsqrt_fusion), kind=kOutput, calls=%fused_computation.39 | convolution fusion | flops 6304805888 | bytes 17577984 | tf_op jit(solution)/shard_map/dot_general | solution.py:237
  98.3 0.0 copy-done.3
  98.3 1.4 fusion.7
  99.6 0.6 pad_maximum_fusion
  100.2 15.8 %shard_map.78 = f32[16,3072]{1,0:T(8,128)} custom-call(f32[1,3072]{1,0:T(1,128)} %bitcast.29), custom_call_target="tpu_custom_call" | custom-call | tf_op jit(solution)/shard_map/pallas_call | solution.py:220
  116.1 1.0 reshape.35
  117.1 0.2 fusion.14
  118.0 0.6 broadcast_in_dim.30.x_ref
  118.6 15.5 %shard_map.79 = f32[32,1536]{1,0:T(8,128)} custom-call(f32[1,1536]{1,0:T(1,128)} %broadcast_in_dim.30.x_ref), custom_call_target="tpu_custom_call" | custom-call | tf_op jit(solution)/shard_map/pallas_call | solution.py:220
  134.1 1.1 reshape.36
  135.2 0.2 fusion.13
  135.3 0.0 copy-done.1
  135.3 4.5 %gather_fusion.1 = f32[768]{0:T(1024)S(1)} fusion(f32[24576]{0:T(1024)S(1)} %bitcast.28, s32[1024]{0:T(1024)S(1)} %pad_clamp_fusion), kind=kCustom, calls=%fused_computation.1.clone | custom fusion | bytes 9216 | tf_op jit(solution)/shard_map/jit(_take)/gather | solution.py:259
  139.8 0.6 broadcast_select_fusion
  140.4 4.5 %gather_fusion = f32[768]{0:T(1024)S(1)} fusion(f32[24576]{0:T(1024)S(1)} %bitcast.27, s32[1024]{0:T(1024)S(1)} %pad_clamp_fusion), kind=kCustom, calls=%fused_computation.clone | custom fusion | bytes 9216 | tf_op jit(solution)/shard_map/jit(_take)/gather | solution.py:259
  144.9 0.6 broadcast_select_fusion.1
  (8 shorter events, 0.1 us)
Async XLA Ops:
  0.6 87.0 %copy-start.2 = (bf16[4096]{0:T(1024)(128)(2,1)S(1)}, bf16[4096]{0:T(1024)(128)(2,1)}, u32[]{:S(2)}) copy-start(bf16[4096]{0:T(1024)(128)(2,1)} %param.11) | copy-start | bytes 24580
  83.3 4.6 %copy-start = (bf16[768,4096]{1,0:T(8,128)(2,1)S(1)}, bf16[768,4096]{1,0:T(8,128)(2,1)}, u32[]{:S(2)}) copy-start(bf16[768,4096]{1,0:T(8,128)(2,1)} %get-tuple-element.5) | copy-start | bytes 18874372
  87.9 10.3 %copy-start.3 = (s32[768]{0:T(1024)S(1)}, s32[768]{0:T(1024)}, u32[]{:S(2)}) copy-start(s32[768]{0:T(1024)} %param.9) | copy-start | bytes 9220
  88.0 47.4 %copy-start.1 = (s32[768]{0:T(1024)S(1)}, s32[768]{0:T(1024)}, u32[]{:S(2)}) copy-start(s32[768]{0:T(1024)} %param.13) | copy-start | bytes 9220

commit v5 on v4

--- a/solution.py
+++ b/solution.py
@@ -33,7 +33,7 @@
     for k in range(1, n):
         copy = pltpu.make_async_remote_copy(
             src_ref=x_ref,
-            dst_ref=o_ref.at[pl.ds(me, 1)],
+            dst_ref=o_ref.at[me],
             send_sem=send_sem.at[k],
             recv_sem=recv_sem.at[k],
             device_id=dev(lax.rem(me + k, n)),
@@ -41,12 +41,12 @@
         )
         copy.start()
         copies.append(copy)
-    o_ref[pl.ds(me, 1), :] = x_ref[...]
+    o_ref[me] = x_ref[...]
     for k in range(1, n):
         source = lax.rem(me + n - k, n)
         incoming = pltpu.make_async_remote_copy(
             src_ref=x_ref,
-            dst_ref=o_ref.at[pl.ds(source, 1)],
+            dst_ref=o_ref.at[source],
             send_sem=send_sem.at[k],
             recv_sem=recv_sem.at[k],
             device_id=dev(source),
@@ -215,16 +215,15 @@
     return full_rows, full_head.reshape(n_x * n_z * depth, vocab)
 
 
-def share(row, axis, other, n, collective_id):
-    width = row.shape[1]
+def share(block, axis, other, n, collective_id):
     return pl.pallas_call(
         functools.partial(_share_kernel, axis, other, n),
-        out_shape=jax.ShapeDtypeStruct((n, width), row.dtype),
+        out_shape=jax.ShapeDtypeStruct((n,) + block.shape, block.dtype),
         in_specs=[pl.BlockSpec(memory_space=pltpu.VMEM)],
         out_specs=pl.BlockSpec(memory_space=pltpu.VMEM),
         scratch_shapes=[pltpu.SemaphoreType.DMA((n,)), pltpu.SemaphoreType.DMA((n,))],
         compiler_params=pltpu.CompilerParams(collective_id=collective_id, has_side_effects=True),
-    )(row)
+    )(block)
 
 
 def local(hidden, targets, row_count, norm_gain, head_weight, return_from, *, n_voc, n_grp, n_x, n_z):
@@ -241,7 +240,7 @@
     weighted = jnp.sum(shifted * logits, axis=1)
     global_columns = lax.axis_index("voc") * vocab_local + jnp.arange(vocab_local, dtype=jnp.int32)
     picked = jnp.sum(jnp.where(global_columns[None, :] == targets[:, None], logits, 0.0), axis=1)
-    stats = jnp.concatenate([peak, total, weighted, picked])[None, :]
+    stats = jnp.concatenate([peak, total, weighted, picked]).reshape(8, -1)
     parts = share(stats, "voc", "grp", n_voc, 0).reshape(n_voc, 4, tok_rows)
     peaks, totals, weights, picks = parts[:, 0], parts[:, 1], parts[:, 2], parts[:, 3]
     peak_all = jnp.max(peaks, axis=0)
@@ -252,11 +251,11 @@
     log_total = peak_all + jnp.log(total_all)
     logp = jnp.where(live_rows, picked_all - log_total, 0.0)
     entropy = jnp.where(live_rows, log_total - weighted_all / total_all, 0.0)
-    results = share(jnp.concatenate([logp, entropy])[None, :], "grp", "voc", n_grp, 1)
-    results = results.reshape(n_grp, 2, tok_rows)
-    every_logp = results[:, 0].reshape(n_grp * tok_rows)
-    every_entropy = results[:, 1].reshape(n_grp * tok_rows)
-    return (jnp.take(every_logp, return_from, axis=0), jnp.take(every_entropy, return_from, axis=0))
+    both = jnp.concatenate([logp, entropy]).reshape(-1, 128)
+    results = share(both, "grp", "voc", n_grp, 1).reshape(n_grp, 2, tok_rows)
+    every = jnp.transpose(results, (0, 2, 1)).reshape(n_grp * tok_rows, 2)
+    picked_rows = jnp.take(every, return_from, axis=0)
+    return (picked_rows[:, 0], picked_rows[:, 1])
 
 
 def solution(mesh):

time: 146 us -> 150 us (1.027)
  local copies, waits for them, and re-layouts: 13.9 us -> 18.2 us
    transpose x0 -> x1, local copies, waits for them, and re-layouts: none -> 6.76 us  [local(): every = jnp.transpose(results, (0, 2, 1)).reshape(n_grp * tok_rows, 2)]
    gather x2 -> x1, local copies, waits for them, and re-layouts: 8.92 us -> 6.14 us  [local(): picked_rows = jnp.take(every, return_from, axis=0)]
where the time goes in v5:
time: 150 us; the launch traced here: 149 us
  Pallas kernels  112 us (75%)
  local copies, waits for them, and re-layouts  18.2 us (12%)
  matrix products  10.1 us (7%)
  other arithmetic  7.22 us (5%)
    pallas_call x1, Pallas kernels, gather_both(): pl.pallas_call(functools.partial(_gather_kernel, n_x, n_z, n_y), out_shap...  80.9 us
    pallas_call x2, Pallas kernels, share(): pl.pallas_call(functools.partial(_share_kernel, axis, other, n), out_shap...  31.3 us
    dot_general x1, matrix products, local(): logits = jnp.dot(normed, piece, preferred_element_type=jnp.float32)  10.1 us
    transpose x1, local copies, waits for them, and re-layouts, local(): every = jnp.transpose(results, (0, 2, 1)).reshape(n_grp * tok_rows, 2)  6.76 us
    gather x1, local copies, waits for them, and re-layouts, local(): picked_rows = jnp.take(every, return_from, axis=0)  6.14 us
    reduce_sum x1, other arithmetic, normalize(): jnp.mean(values * values, axis=1, keepdims=True) + EPSILON  4.22 us

profile of v5, /device:TPU:1, one launch (start us, length us, event | category | flops | bytes accessed | tf_op | source)
XLA Modules:
  0.0 149.2 jit_solution(11577944506989173871)
XLA Ops:
  0.6 0.0 copy-start.2
  0.6 1.8 %copy.12.head_ref = bf16[128,1000]{1,0:T(8,128)(2,1)} copy(bf16[128,1000]{0,1:T(8,128)(2,1)} %param.10) | data formatting | bytes 512000 | tf_op args[4]
  2.5 80.9 %shard_map.77 = (bf16[768,4096]{1,0:T(8,128)(2,1)}, bf16[4,8,128,1000]{3,2,1,0:T(8,128)(2,1)}) custom-call(bf16[768,256]{1,0:T(8,128)(2,1)} %rows_ref.1, bf16[128,1000]{1,0:T(8,128)(2,1)} %copy.12.head_ref), custom_call_target="tpu_custom_call" | custom-call | tf_op jit(solution)/shard_map/pallas_call | solution.py:205
  83.3 0.0 copy-start
  83.4 4.2 %fusion = f32[768]{0:T(1024)S(1)} fusion(bf16[768,4096]{1,0:T(8,128)(2,1)} %get-tuple-element.4), kind=kLoop, calls=%fused_computation.3 | loop fusion | flops 9436416 | bytes 6294528 | tf_op jit(solution)/shard_map/reduce_sum | solution.py:17
  87.6 0.0 copy-done.2
  87.6 0.3 copy-done
  87.9 0.0 copy-start.3
  88.0 10.1 %fusion.14 = (f32[768]{0:T(1024)S(1)}, f32[768,1000]{0,1:T(8,128)S(1)}) fusion(bf16[4096,1000]{1,0:T(8,128)(2,1)} %bitcast.32, bf16[768,4096]{1,0:T(8,128)(2,1)S(1)} %copy-done, f32[4096]{0:T(1024)S(1)} %convert_element_type.10, f32[768]{0:T(1024)S(1)} %add_rsqrt_fusion), kind=kOutput, calls=%fused_computation.38 | convolution fusion | flops 6304805888 | bytes 17577984 | tf_op jit(solution)/shard_map/dot_general | solution.py:236
  98.1 0.0 copy-done.3
  98.1 1.4 fusion.7
  99.5 0.6 pad_maximum_fusion.x_ref
  100.1 15.8 %shard_map.78 = f32[16,8,384]{2,1,0:T(8,128)} custom-call(f32[8,384]{1,0:T(8,128)} %pad_maximum_fusion.x_ref), custom_call_target="tpu_custom_call" | custom-call | tf_op jit(solution)/shard_map/pallas_call | solution.py:219
  116.0 1.0 reshape.59
  117.0 0.2 fusion.13
  117.9 0.6 pad_maximum_fusion.1.x_ref
  118.5 15.5 %shard_map.79 = f32[32,12,128]{2,1,0:T(8,128)} custom-call(f32[12,128]{1,0:T(8,128)} %pad_maximum_fusion.1.x_ref), custom_call_target="tpu_custom_call" | custom-call | tf_op jit(solution)/shard_map/pallas_call | solution.py:219
  134.0 1.1 reshape.60
  135.1 0.0 copy-start.1
  135.1 6.8 %copy.15 = f32[32,768,2]{2,1,0:T(8,128)} copy(f32[32,768,2]{1,2,0:T(2,128)S(1)} %bitcast.31) | data formatting | bytes 393216 | tf_op jit(solution)/shard_map/transpose | solution.py:256
  141.8 0.0 copy-done.1
  141.9 6.1 %gather_fusion = f32[768,2]{1,0:T(8,128)S(1)} fusion(f32[24576,2]{1,0:T(8,128)} %bitcast.30, s32[1024]{0:T(1024)S(1)} %pad_clamp_fusion), kind=kCustom, calls=%fused_computation | custom fusion | bytes 15360 | tf_op jit(solution)/shard_map/jit(_take)/gather | solution.py:257
  148.0 0.2 broadcast_select_fusion
  148.2 1.0 slice_reduce_fusion
  (12 shorter events, 0.1 us)
Async XLA Ops:
  0.6 87.0 %copy-start.2 = (bf16[4096]{0:T(1024)(128)(2,1)S(1)}, bf16[4096]{0:T(1024)(128)(2,1)}, u32[]{:S(2)}) copy-start(bf16[4096]{0:T(1024)(128)(2,1)} %param.9) | copy-start | bytes 24580
  83.3 4.6 %copy-start = (bf16[768,4096]{1,0:T(8,128)(2,1)S(1)}, bf16[768,4096]{1,0:T(8,128)(2,1)}, u32[]{:S(2)}) copy-start(bf16[768,4096]{1,0:T(8,128)(2,1)} %get-tuple-element.4) | copy-start | bytes 18874372
  87.9 10.2 %copy-start.3 = (s32[768]{0:T(1024)S(1)}, s32[768]{0:T(1024)}, u32[]{:S(2)}) copy-start(s32[768]{0:T(1024)} %param.7) | copy-start | bytes 9220
  135.1 6.8 %copy-start.1 = (s32[768]{0:T(1024)S(1)}, s32[768]{0:T(1024)}, u32[]{:S(2)}) copy-start(s32[768]{0:T(1024)} %param.11) | copy-start | bytes 9220

commit v6 on v5

--- a/solution.py
+++ b/solution.py
@@ -61,49 +61,53 @@
         self.pos, self.n, self.device, self.slot, self.own = pos, n, device, slot, own
         self.sems = sems
         self.on_arrival = on_arrival
-        self.right = n // 2
-        self.left = n - 1 - self.right
+        self.steps = n // 2
+        self.split = n % 2 == 0
         self.copies = []
 
-    def _copy(self, origin, kind, s, target):
-        view = self.slot(origin)
-        return pltpu.make_async_remote_copy(
-            src_ref=view, dst_ref=view,
-            send_sem=self.sems.at[kind, s], recv_sem=self.sems.at[kind + 1, s],
-            device_id=self.device(target), device_id_type=MESH,
-        )
+    def _part(self, s, kind):
+        return kind // 2 if self.split and s == self.steps else None
 
     def _origin(self, step, sign):
         return lax.rem(self.pos + sign * step + 2 * self.n, self.n)
 
+    def _desc(self, src, origin, kind, s, target):
+        return pltpu.make_async_remote_copy(
+            src_ref=src, dst_ref=self.slot(origin, self._part(s, kind)),
+            send_sem=self.sems.at[kind, s - 1], recv_sem=self.sems.at[kind + 1, s - 1],
+            device_id=self.device(target), device_id_type=MESH,
+        )
+
     def step(self, s):
-        for count, kind, sign in ((self.right, 0, 1), (self.left, 2, -1)):
-            if s > count:
-                continue
+        if s > self.steps:
+            return
+        for kind, sign in ((0, 1), (2, -1)):
             target = self._origin(1, sign)
             origin = self._origin(s - 1, -sign)
+            part = self._part(s, kind)
             if s == 1:
-                src = self.own
+                src = self.own(part)
             else:
-                self._copy(origin, kind, s - 2, target).wait_recv()
+                self._desc(self.slot(origin), origin, kind, s - 1, target).wait_recv()
                 if self.on_arrival is not None:
                     self.on_arrival(origin)
-                src = self.slot(origin)
-            copy = pltpu.make_async_remote_copy(
-                src_ref=src, dst_ref=self.slot(origin),
-                send_sem=self.sems.at[kind, s - 1], recv_sem=self.sems.at[kind + 1, s - 1],
-                device_id=self.device(target), device_id_type=MESH,
-            )
+                src = self.slot(origin, part)
+            copy = self._desc(src, origin, kind, s, target)
             copy.start()
             self.copies.append(copy)
 
     def finish_recv(self):
-        for count, kind, sign in ((self.right, 0, 1), (self.left, 2, -1)):
-            if count:
-                origin = self._origin(count, -sign)
-                self._copy(origin, kind, count - 1, self._origin(1, sign)).wait_recv()
-                if self.on_arrival is not None:
-                    self.on_arrival(origin)
+        if not self.steps:
+            return
+        last = []
+        for kind, sign in ((0, 1), (2, -1)):
+            origin = self._origin(self.steps, -sign)
+            view = self.slot(origin, self._part(self.steps, kind))
+            self._desc(view, origin, kind, self.steps, self._origin(1, sign)).wait_recv()
+            last.append(origin)
+        if self.on_arrival is not None:
+            for origin in last[:1] if self.split else last:
+                self.on_arrival(origin)
 
     def finish_send(self):
         for copy in self.copies:
@@ -163,9 +167,18 @@
     copy.start()
     pair_copies.append(copy)
     rows_out[:, cols(v)] = rows_ref[...]
-    rows = _Ring(y, n_y, along_y, lambda t: rows_out.at[:, cols(t * 2 + c)], rows_ref, sems.at[4], forward)
-    first_x = _Ring(x, n_x, along_x, lambda t: head_out.at[t, z, lo], head_ref.at[lo], sems.at[0])
-    first_z = _Ring(z, n_z, along_z, lambda t: head_out.at[x, t, hi], head_ref.at[hi], sems.at[1])
+    def halves(size, start=0):
+        return lambda part: pl.ds(start, size) if part is None else pl.ds(start + part * (size // 2), size // 2)
+
+    rows_part = halves(rows_ref.shape[0])
+    lo_part, hi_part = halves(half), halves(half, half)
+    x_part, z_part = halves(n_x), halves(n_z)
+    rows = _Ring(y, n_y, along_y, lambda t, p=None: rows_out.at[rows_part(p), cols(t * 2 + c)],
+                 lambda p: rows_ref.at[rows_part(p)], sems.at[4], forward)
+    first_x = _Ring(x, n_x, along_x, lambda t, p=None: head_out.at[t, z, lo_part(p)],
+                    lambda p: head_ref.at[lo_part(p)], sems.at[0])
+    first_z = _Ring(z, n_z, along_z, lambda t, p=None: head_out.at[x, t, hi_part(p)],
+                    lambda p: head_ref.at[hi_part(p)], sems.at[1])
     steps = max(n_x, n_z, n_y)
     rows.step(1)
     for s in range(1, steps):
@@ -174,8 +187,10 @@
     own.wait()
     first_x.finish_recv()
     first_z.finish_recv()
-    second_z = _Ring(z, n_z, along_z, lambda t: head_out.at[:, t, lo], head_out.at[:, z, lo], sems.at[2])
-    second_x = _Ring(x, n_x, along_x, lambda t: head_out.at[t, :, hi], head_out.at[x, :, hi], sems.at[3])
+    second_z = _Ring(z, n_z, along_z, lambda t, p=None: head_out.at[x_part(p), t, lo],
+                     lambda p: head_out.at[x_part(p), z, lo], sems.at[2])
+    second_x = _Ring(x, n_x, along_x, lambda t, p=None: head_out.at[t, z_part(p), hi],
+                     lambda p: head_out.at[x, z_part(p), hi], sems.at[3])
     for s in range(1, steps):
         second_z.step(s)
         second_x.step(s)
@@ -253,9 +268,9 @@
     entropy = jnp.where(live_rows, log_total - weighted_all / total_all, 0.0)
     both = jnp.concatenate([logp, entropy]).reshape(-1, 128)
     results = share(both, "grp", "voc", n_grp, 1).reshape(n_grp, 2, tok_rows)
-    every = jnp.transpose(results, (0, 2, 1)).reshape(n_grp * tok_rows, 2)
-    picked_rows = jnp.take(every, return_from, axis=0)
-    return (picked_rows[:, 0], picked_rows[:, 1])
+    every_logp = results[:, 0].reshape(n_grp * tok_rows)
+    every_entropy = results[:, 1].reshape(n_grp * tok_rows)
+    return (jnp.take(every_logp, return_from, axis=0), jnp.take(every_entropy, return_from, axis=0))
 
 
 def solution(mesh):

time: 150 us -> 141 us (0.940)
  local copies, waits for them, and re-layouts: 18.2 us -> 13.4 us
  Pallas kernels: 112 us -> 108 us
    transpose x1 -> x0, local copies, waits for them, and re-layouts: 6.76 us -> none  [local(): every = jnp.transpose(results, (0, 2, 1)).reshape(n_grp * tok_rows, 2)]
    pallas_call x1, Pallas kernels: 80.9 us -> 78 us  [gather_both(): pl.pallas_call(functools.partial(_gather_kernel, n_x, n_z, n_y), out_shap...]
    gather x1 -> x2, local copies, waits for them, and re-layouts: 6.14 us -> 8.92 us  [the longest x1 4.46 us: local(): jnp.take(every_entropy, return_from, axis=0)]
    pallas_call x2, Pallas kernels: 31.3 us -> 29.5 us  [share(): pl.pallas_call(functools.partial(_share_kernel, axis, other, n), out_shap...]
where the time goes in v6:
time: 141 us
  Pallas kernels  108 us (77%)
  local copies, waits for them, and re-layouts  13.4 us (10%)
  matrix products  10.3 us (7%)
  other arithmetic  8.24 us (6%)
  between operations  1.46 us (1%)
    pallas_call x1, Pallas kernels, gather_both(): pl.pallas_call(functools.partial(_gather_kernel, n_x, n_z, n_y), out_shap...  78 us
    pallas_call x2, Pallas kernels, share(): pl.pallas_call(functools.partial(_share_kernel, axis, other, n), out_shap...  29.5 us
    dot_general x1, matrix products, local(): logits = jnp.dot(normed, piece, preferred_element_type=jnp.float32)  10.3 us
    gather x1, local copies, waits for them, and re-layouts, local(): jnp.take(every_entropy, return_from, axis=0)  4.46 us
    gather x1, local copies, waits for them, and re-layouts, local(): jnp.take(every_logp, return_from, axis=0)  4.45 us
    reduce_sum x1, other arithmetic, normalize(): jnp.mean(values * values, axis=1, keepdims=True) + EPSILON  4.22 us

profile of v6, /device:TPU:1, one launch (start us, length us, event | category | flops | bytes accessed | tf_op | source)
XLA Modules:
  0.0 140.9 jit_solution(1087753642317031388)
XLA Ops:
  0.6 0.0 copy-start.2
  0.6 1.8 %copy.11.head_ref = bf16[128,1000]{1,0:T(8,128)(2,1)} copy(bf16[128,1000]{0,1:T(8,128)(2,1)} %param.12) | data formatting | bytes 512000 | tf_op args[4]
  2.5 78.0 %shard_map.77 = (bf16[768,4096]{1,0:T(8,128)(2,1)}, bf16[4,8,128,1000]{3,2,1,0:T(8,128)(2,1)}) custom-call(bf16[768,256]{1,0:T(8,128)(2,1)} %rows_ref.1, bf16[128,1000]{1,0:T(8,128)(2,1)} %copy.11.head_ref), custom_call_target="tpu_custom_call" | custom-call | tf_op jit(solution)/shard_map/pallas_call | solution.py:220
  80.5 0.0 copy-start
  80.5 4.2 %fusion = f32[768]{0:T(1024)S(1)} fusion(bf16[768,4096]{1,0:T(8,128)(2,1)} %get-tuple-element.5), kind=kLoop, calls=%fused_computation.4 | loop fusion | flops 9436416 | bytes 6294528 | tf_op jit(solution)/shard_map/reduce_sum | solution.py:17
  84.7 0.0 copy-done.2
  84.7 0.3 copy-done
  85.1 0.0 copy-start.3
  85.1 0.0 copy-start.1
  85.1 10.3 %fusion.15 = (f32[768]{0:T(1024)S(1)}, f32[768,1000]{0,1:T(8,128)S(1)}) fusion(bf16[4096,1000]{1,0:T(8,128)(2,1)} %bitcast.32, bf16[768,4096]{1,0:T(8,128)(2,1)S(1)} %copy-done, f32[4096]{0:T(1024)S(1)} %convert_element_type.10, f32[768]{0:T(1024)S(1)} %add_rsqrt_fusion), kind=kOutput, calls=%fused_computation.39 | convolution fusion | flops 6304805888 | bytes 17577984 | tf_op jit(solution)/shard_map/dot_general | solution.py:251
  95.4 0.0 copy-done.3
  95.4 1.4 fusion.7
  96.8 0.6 pad_maximum_fusion.x_ref
  97.4 16.4 %shard_map.78 = f32[16,8,384]{2,1,0:T(8,128)} custom-call(f32[8,384]{1,0:T(8,128)} %pad_maximum_fusion.x_ref), custom_call_target="tpu_custom_call" | custom-call | tf_op jit(solution)/shard_map/pallas_call | solution.py:234
  113.9 1.0 reshape.56
  114.9 0.2 fusion.14
  115.8 0.6 pad_maximum_fusion.1.x_ref
  116.4 13.1 %shard_map.79 = f32[32,12,128]{2,1,0:T(8,128)} custom-call(f32[12,128]{1,0:T(8,128)} %pad_maximum_fusion.1.x_ref), custom_call_target="tpu_custom_call" | custom-call | tf_op jit(solution)/shard_map/pallas_call | solution.py:234
  129.5 1.1 reshape.57
  130.5 0.2 fusion.13
  130.7 0.0 copy-done.1
  130.7 4.5 %gather_fusion.1 = f32[768]{0:T(1024)S(1)} fusion(f32[24576]{0:T(1024)S(1)} %bitcast.31, s32[1024]{0:T(1024)S(1)} %pad_clamp_fusion), kind=kCustom, calls=%fused_computation.1.clone | custom fusion | bytes 9216 | tf_op jit(solution)/shard_map/jit(_take)/gather | solution.py:273
  135.2 0.6 broadcast_select_fusion
  135.8 4.5 %gather_fusion = f32[768]{0:T(1024)S(1)} fusion(f32[24576]{0:T(1024)S(1)} %bitcast.30, s32[1024]{0:T(1024)S(1)} %pad_clamp_fusion), kind=kCustom, calls=%fused_computation.clone | custom fusion | bytes 9216 | tf_op jit(solution)/shard_map/jit(_take)/gather | solution.py:273
  140.3 0.6 broadcast_select_fusion.1
  (11 shorter events, 0.1 us)
Async XLA Ops:
  0.6 84.1 %copy-start.2 = (bf16[4096]{0:T(1024)(128)(2,1)S(1)}, bf16[4096]{0:T(1024)(128)(2,1)}, u32[]{:S(2)}) copy-start(bf16[4096]{0:T(1024)(128)(2,1)} %param.11) | copy-start | bytes 24580
  80.5 4.6 %copy-start = (bf16[768,4096]{1,0:T(8,128)(2,1)S(1)}, bf16[768,4096]{1,0:T(8,128)(2,1)}, u32[]{:S(2)}) copy-start(bf16[768,4096]{1,0:T(8,128)(2,1)} %get-tuple-element.5) | copy-start | bytes 18874372
  85.1 10.3 %copy-start.3 = (s32[768]{0:T(1024)S(1)}, s32[768]{0:T(1024)}, u32[]{:S(2)}) copy-start(s32[768]{0:T(1024)} %param.9) | copy-start | bytes 9220
  85.1 45.6 %copy-start.1 = (s32[768]{0:T(1024)S(1)}, s32[768]{0:T(1024)}, u32[]{:S(2)}) copy-start(s32[768]{0:T(1024)} %param.13) | copy-start | bytes 9220

commit v7 on v6

--- a/solution.py
+++ b/solution.py
@@ -268,9 +268,17 @@
     entropy = jnp.where(live_rows, log_total - weighted_all / total_all, 0.0)
     both = jnp.concatenate([logp, entropy]).reshape(-1, 128)
     results = share(both, "grp", "voc", n_grp, 1).reshape(n_grp, 2, tok_rows)
-    every_logp = results[:, 0].reshape(n_grp * tok_rows)
-    every_entropy = results[:, 1].reshape(n_grp * tok_rows)
-    return (jnp.take(every_logp, return_from, axis=0), jnp.take(every_entropy, return_from, axis=0))
+    lanes = 128
+    every = jnp.concatenate(
+        [results[:, 0].reshape(-1, lanes), results[:, 1].reshape(-1, lanes)], axis=1)
+    high = return_from // lanes
+    low = return_from % lanes
+    pick_row = (high[:, None] == jnp.arange(every.shape[0], dtype=jnp.int32)[None, :]).astype(jnp.float32)
+    rows_picked = jnp.dot(pick_row, every, precision=lax.Precision.HIGHEST)
+    pick_lane = low[:, None] == jnp.arange(lanes, dtype=jnp.int32)[None, :]
+    token_logp = jnp.sum(jnp.where(pick_lane, rows_picked[:, :lanes], 0.0), axis=1)
+    token_entropy = jnp.sum(jnp.where(pick_lane, rows_picked[:, lanes:], 0.0), axis=1)
+    return (token_logp, token_entropy)
 
 
 def solution(mesh):

time: 141 us -> 132 us (0.936)
  local copies, waits for them, and re-layouts: 13.4 us -> 4.45 us
    gather x2 -> x0, local copies, waits for them, and re-layouts: 8.92 us -> none  [the longest x1 4.46 us: local(): jnp.take(every_entropy, return_from, axis=0)]
where the time goes in v7:
time: 132 us
  Pallas kernels  108 us (82%)
  matrix products  11 us (8%)
  other arithmetic  7.72 us (6%)
  local copies, waits for them, and re-layouts  4.45 us (3%)
  between operations  1.44 us (1%)
    pallas_call x1, Pallas kernels, gather_both(): pl.pallas_call(functools.partial(_gather_kernel, n_x, n_z, n_y), out_shap...  78 us
    pallas_call x2, Pallas kernels, share(): pl.pallas_call(functools.partial(_share_kernel, axis, other, n), out_shap...  29.5 us
    dot_general x1, matrix products, local(): logits = jnp.dot(normed, piece, preferred_element_type=jnp.float32)  10.3 us
    reduce_sum x1, other arithmetic, normalize(): jnp.mean(values * values, axis=1, keepdims=True) + EPSILON  4.22 us

profile of v7, /device:TPU:1, one launch (start us, length us, event | category | flops | bytes accessed | tf_op | source)
XLA Modules:
  0.0 132.1 jit_solution(15636394448863173613)
XLA Ops:
  0.6 0.0 copy-start.1
  0.6 1.8 %copy.11.head_ref = bf16[128,1000]{1,0:T(8,128)(2,1)} copy(bf16[128,1000]{0,1:T(8,128)(2,1)} %param.10) | data formatting | bytes 512000 | tf_op args[4]
  2.5 78.0 %shard_map.77 = (bf16[768,4096]{1,0:T(8,128)(2,1)}, bf16[4,8,128,1000]{3,2,1,0:T(8,128)(2,1)}) custom-call(bf16[768,256]{1,0:T(8,128)(2,1)} %rows_ref.1, bf16[128,1000]{1,0:T(8,128)(2,1)} %copy.11.head_ref), custom_call_target="tpu_custom_call" | custom-call | tf_op jit(solution)/shard_map/pallas_call | solution.py:220
  80.5 0.0 copy-start
  80.5 4.2 %fusion = f32[768]{0:T(1024)S(1)} fusion(bf16[768,4096]{1,0:T(8,128)(2,1)} %get-tuple-element.4), kind=kLoop, calls=%fused_computation.2 | loop fusion | flops 9436416 | bytes 6294528 | tf_op jit(solution)/shard_map/reduce_sum | solution.py:17
  84.7 0.0 copy-done.1
  84.7 0.3 copy-done
  85.1 0.0 copy-start.2
  85.1 0.0 copy-start.3
  85.1 10.3 %fusion.25 = (f32[768]{0:T(1024)S(1)}, f32[768,1000]{0,1:T(8,128)S(1)}) fusion(bf16[4096,1000]{1,0:T(8,128)(2,1)} %bitcast.32, bf16[768,4096]{1,0:T(8,128)(2,1)S(1)} %copy-done, f32[4096]{0:T(1024)S(1)} %convert_element_type.11, f32[768]{0:T(1024)S(1)} %add_rsqrt_fusion), kind=kOutput, calls=%fused_computation.52 | convolution fusion | flops 6304805888 | bytes 17577984 | tf_op jit(solution)/shard_map/dot_general | solution.py:251
  95.4 0.0 copy-done.2
  95.4 1.4 %fusion.7 = (f32[768]{0:T(1024)S(1)}, f32[768]{0:T(1024)S(1)}, f32[768]{0:T(1024)S(1)}) fusion(f32[768,1000]{0,1:T(8,128)S(1)} %get-tuple-element.27, f32[768]{0:T(1024)S(1)} %get-tuple-element.26, s32[768]{0:T(1024)S(1)} %copy-done.2, s32[1000]{0:T(1024)S(1)} %iota_add_fusion), kind=kLoop, calls=%fused_computation.11 | loop fusion | flops 5373696 | bytes 3091360 | tf_op jit(solution)/shard_map/reduce_sum | solution.py:254
  96.8 0.6 pad_maximum_fusion.x_ref
  97.4 16.4 %shard_map.78 = f32[16,8,384]{2,1,0:T(8,128)} custom-call(f32[8,384]{1,0:T(8,128)} %pad_maximum_fusion.x_ref), custom_call_target="tpu_custom_call" | custom-call | tf_op jit(solution)/shard_map/pallas_call | solution.py:234
  113.9 1.0 reshape.53
  114.9 0.2 fusion.24
  115.8 0.6 pad_maximum_fusion.1.x_ref
  116.4 13.1 %shard_map.79 = f32[32,12,128]{2,1,0:T(8,128)} custom-call(f32[12,128]{1,0:T(8,128)} %pad_maximum_fusion.1.x_ref), custom_call_target="tpu_custom_call" | custom-call | tf_op jit(solution)/shard_map/pallas_call | solution.py:234
  129.5 1.1 reshape.54
  130.5 0.2 fusion.23
  130.7 0.0 copy-done.3
  130.7 0.7 fusion.8
  131.5 0.7 fusion.9
  (10 shorter events, 0.1 us)
Async XLA Ops:
  0.6 84.1 %copy-start.1 = (bf16[4096]{0:T(1024)(128)(2,1)S(1)}, bf16[4096]{0:T(1024)(128)(2,1)}, u32[]{:S(2)}) copy-start(bf16[4096]{0:T(1024)(128)(2,1)} %param.9) | copy-start | bytes 24580
  80.5 4.6 %copy-start = (bf16[768,4096]{1,0:T(8,128)(2,1)S(1)}, bf16[768,4096]{1,0:T(8,128)(2,1)}, u32[]{:S(2)}) copy-start(bf16[768,4096]{1,0:T(8,128)(2,1)} %get-tuple-element.4) | copy-start | bytes 18874372
  85.1 10.3 %copy-start.2 = (s32[768]{0:T(1024)S(1)}, s32[768]{0:T(1024)}, u32[]{:S(2)}) copy-start(s32[768]{0:T(1024)} %param.7) | copy-start | bytes 9220
  85.1 45.6 %copy-start.3 = (s32[768]{0:T(1024)S(1)}, s32[768]{0:T(1024)}, u32[]{:S(2)}) copy-start(s32[768]{0:T(1024)} %param.11) | copy-start | bytes 9220

commit v8 on v7

--- a/solution.py
+++ b/solution.py
@@ -64,6 +64,12 @@
         self.steps = n // 2
         self.split = n % 2 == 0
         self.copies = []
+        self.next = 1
+
+    def advance(self):
+        if self.next <= self.steps:
+            self.step(self.next)
+            self.next += 1
 
     def _part(self, s, kind):
         return kind // 2 if self.split and s == self.steps else None
@@ -97,6 +103,8 @@
             self.copies.append(copy)
 
     def finish_recv(self):
+        while self.next <= self.steps:
+            self.advance()
         if not self.steps:
             return
         last = []
@@ -179,23 +187,30 @@
                     lambda p: head_ref.at[lo_part(p)], sems.at[0])
     first_z = _Ring(z, n_z, along_z, lambda t, p=None: head_out.at[x, t, hi_part(p)],
                     lambda p: head_ref.at[hi_part(p)], sems.at[1])
-    steps = max(n_x, n_z, n_y)
-    rows.step(1)
-    for s in range(1, steps):
-        first_x.step(s)
-        first_z.step(s)
+    rows.advance()
+    first_x.advance()
+    first_z.advance()
+    first_x.advance()
+    first_z.advance()
     own.wait()
     first_x.finish_recv()
-    first_z.finish_recv()
     second_z = _Ring(z, n_z, along_z, lambda t, p=None: head_out.at[x_part(p), t, lo],
                      lambda p: head_out.at[x_part(p), z, lo], sems.at[2])
     second_x = _Ring(x, n_x, along_x, lambda t, p=None: head_out.at[t, z_part(p), hi],
                      lambda p: head_out.at[x, z_part(p), hi], sems.at[3])
-    for s in range(1, steps):
-        second_z.step(s)
-        second_x.step(s)
-        rows.step(s + 1)
+    second_z.advance()
+    first_z.advance()
+    rows.advance()
+    first_z.advance()
+    first_z.finish_recv()
+    second_x.advance()
+    rows.advance()
+    second_z.advance()
+    rows.advance()
+    second_z.advance()
     rows.finish_recv()
+    second_x.advance()
+    second_z.advance()
     second_z.finish_recv()
     second_x.finish_recv()
     for t in range(n_y):

time: 132 us -> 134 us (1.015)
  no operation moved by 1% of the time
where the time goes in v8:
time: 134 us; the launch traced here: 133 us
  Pallas kernels  109 us (81%)
  matrix products  11 us (8%)
  other arithmetic  7.72 us (6%)
  local copies, waits for them, and re-layouts  4.45 us (3%)
  between operations  1.44 us (1%)
    pallas_call x1, Pallas kernels, gather_both(): pl.pallas_call(functools.partial(_gather_kernel, n_x, n_z, n_y), out_shap...  79.1 us
    pallas_call x2, Pallas kernels, share(): pl.pallas_call(functools.partial(_share_kernel, axis, other, n), out_shap...  29.6 us
    dot_general x1, matrix products, local(): logits = jnp.dot(normed, piece, preferred_element_type=jnp.float32)  10.3 us
    reduce_sum x1, other arithmetic, normalize(): jnp.mean(values * values, axis=1, keepdims=True) + EPSILON  4.22 us

profile of v8, /device:TPU:1, one launch (start us, length us, event | category | flops | bytes accessed | tf_op | source)
XLA Modules:
  0.0 133.2 jit_solution(18033096943116230994)
XLA Ops:
  0.6 0.0 copy-start.1
  0.6 1.8 %copy.11.head_ref = bf16[128,1000]{1,0:T(8,128)(2,1)} copy(bf16[128,1000]{0,1:T(8,128)(2,1)} %param.10) | data formatting | bytes 512000 | tf_op args[4]
  2.5 79.1 %shard_map.77 = (bf16[768,4096]{1,0:T(8,128)(2,1)}, bf16[4,8,128,1000]{3,2,1,0:T(8,128)(2,1)}) custom-call(bf16[768,256]{1,0:T(8,128)(2,1)} %rows_ref.1, bf16[128,1000]{1,0:T(8,128)(2,1)} %copy.11.head_ref), custom_call_target="tpu_custom_call" | custom-call | tf_op jit(solution)/shard_map/pallas_call | solution.py:235
  81.6 0.0 copy-start
  81.6 4.2 %fusion = f32[768]{0:T(1024)S(1)} fusion(bf16[768,4096]{1,0:T(8,128)(2,1)} %get-tuple-element.4), kind=kLoop, calls=%fused_computation.2 | loop fusion | flops 9436416 | bytes 6294528 | tf_op jit(solution)/shard_map/reduce_sum | solution.py:17
  85.8 0.0 copy-done.1
  85.8 0.3 copy-done
  86.2 0.0 copy-start.2
  86.2 0.0 copy-start.3
  86.2 10.3 %fusion.25 = (f32[768]{0:T(1024)S(1)}, f32[768,1000]{0,1:T(8,128)S(1)}) fusion(bf16[4096,1000]{1,0:T(8,128)(2,1)} %bitcast.32, bf16[768,4096]{1,0:T(8,128)(2,1)S(1)} %copy-done, f32[4096]{0:T(1024)S(1)} %convert_element_type.11, f32[768]{0:T(1024)S(1)} %add_rsqrt_fusion), kind=kOutput, calls=%fused_computation.52 | convolution fusion | flops 6304805888 | bytes 17577984 | tf_op jit(solution)/shard_map/dot_general | solution.py:266
  96.5 0.0 copy-done.2
  96.5 1.4 %fusion.7 = (f32[768]{0:T(1024)S(1)}, f32[768]{0:T(1024)S(1)}, f32[768]{0:T(1024)S(1)}) fusion(f32[768,1000]{0,1:T(8,128)S(1)} %get-tuple-element.27, f32[768]{0:T(1024)S(1)} %get-tuple-element.26, s32[768]{0:T(1024)S(1)} %copy-done.2, s32[1000]{0:T(1024)S(1)} %iota_add_fusion), kind=kLoop, calls=%fused_computation.11 | loop fusion | flops 5373696 | bytes 3091360 | tf_op jit(solution)/shard_map/reduce_sum | solution.py:269
  97.9 0.6 pad_maximum_fusion.x_ref
  98.5 15.8 %shard_map.78 = f32[16,8,384]{2,1,0:T(8,128)} custom-call(f32[8,384]{1,0:T(8,128)} %pad_maximum_fusion.x_ref), custom_call_target="tpu_custom_call" | custom-call | tf_op jit(solution)/shard_map/pallas_call | solution.py:249
  114.3 1.0 reshape.53
  115.3 0.2 fusion.24
  116.2 0.6 pad_maximum_fusion.1.x_ref
  116.8 13.8 %shard_map.79 = f32[32,12,128]{2,1,0:T(8,128)} custom-call(f32[12,128]{1,0:T(8,128)} %pad_maximum_fusion.1.x_ref), custom_call_target="tpu_custom_call" | custom-call | tf_op jit(solution)/shard_map/pallas_call | solution.py:249
  130.6 1.1 reshape.54
  131.7 0.2 fusion.23
  131.8 0.0 copy-done.3
  131.8 0.7 fusion.8
  132.6 0.7 fusion.9
  (10 shorter events, 0.1 us)
Async XLA Ops:
  0.6 85.2 %copy-start.1 = (bf16[4096]{0:T(1024)(128)(2,1)S(1)}, bf16[4096]{0:T(1024)(128)(2,1)}, u32[]{:S(2)}) copy-start(bf16[4096]{0:T(1024)(128)(2,1)} %param.9) | copy-start | bytes 24580
  81.6 4.6 %copy-start = (bf16[768,4096]{1,0:T(8,128)(2,1)S(1)}, bf16[768,4096]{1,0:T(8,128)(2,1)}, u32[]{:S(2)}) copy-start(bf16[768,4096]{1,0:T(8,128)(2,1)} %get-tuple-element.4) | copy-start | bytes 18874372
  86.2 10.3 %copy-start.2 = (s32[768]{0:T(1024)S(1)}, s32[768]{0:T(1024)}, u32[]{:S(2)}) copy-start(s32[768]{0:T(1024)} %param.7) | copy-start | bytes 9220
  86.2 45.7 %copy-start.3 = (s32[768]{0:T(1024)S(1)}, s32[768]{0:T(1024)}, u32[]{:S(2)}) copy-start(s32[768]{0:T(1024)} %param.11) | copy-start | bytes 9220

commit v9 on v8

--- a/solution.py
+++ b/solution.py
@@ -18,42 +18,74 @@
     return (values * scale * norm_gain.astype(jnp.float32)[None, :]).astype(jnp.bfloat16)
 
 
-def _share_kernel(axis, other, n, x_ref, o_ref, send_sem, recv_sem):
-    me = lax.axis_index(axis)
-    fixed = lax.axis_index(other)
-
-    def dev(t):
-        return (fixed, t) if axis == "voc" else (t, fixed)
+def _exchange_kernel(n_voc, n_grp, stats_ref, live_ref, out_ref, parts, voc_sems, grp_sems):
+    g = lax.axis_index("grp")
+    v = lax.axis_index("voc")
+
+    def along_voc(t):
+        return (g, t)
+
+    def along_grp(t):
+        return (t, v)
 
     barrier = pltpu.get_barrier_semaphore()
-    for k in range(1, n):
-        pl.semaphore_signal(barrier, inc=1, device_id=dev(lax.rem(me + k, n)), device_id_type=MESH)
-    pl.semaphore_wait(barrier, n - 1)
-    copies = []
-    for k in range(1, n):
-        copy = pltpu.make_async_remote_copy(
-            src_ref=x_ref,
-            dst_ref=o_ref.at[me],
-            send_sem=send_sem.at[k],
-            recv_sem=recv_sem.at[k],
-            device_id=dev(lax.rem(me + k, n)),
-            device_id_type=MESH,
-        )
-        copy.start()
-        copies.append(copy)
-    o_ref[me] = x_ref[...]
-    for k in range(1, n):
-        source = lax.rem(me + n - k, n)
-        incoming = pltpu.make_async_remote_copy(
-            src_ref=x_ref,
-            dst_ref=o_ref.at[source],
-            send_sem=send_sem.at[k],
-            recv_sem=recv_sem.at[k],
-            device_id=dev(source),
-            device_id_type=MESH,
-        )
-        copies[k - 1].wait_send()
-        incoming.wait_recv()
+    for k in range(1, n_voc):
+        pl.semaphore_signal(barrier, inc=1, device_id=along_voc(lax.rem(v + k, n_voc)), device_id_type=MESH)
+    for k in range(1, n_grp):
+        pl.semaphore_signal(barrier, inc=1, device_id=along_grp(lax.rem(g + k, n_grp)), device_id_type=MESH)
+    pl.semaphore_wait(barrier, n_voc + n_grp - 2)
+
+    def send_all(src, buffer, me, n, sems, device, fill):
+        copies = []
+        for k in range(1, n):
+            copy = pltpu.make_async_remote_copy(
+                src_ref=src, dst_ref=buffer.at[me],
+                send_sem=sems.at[0, k], recv_sem=sems.at[1, k],
+                device_id=device(lax.rem(me + k, n)), device_id_type=MESH,
+            )
+            copy.start()
+            copies.append(copy)
+        fill()
+        for k in range(1, n):
+            source = lax.rem(me + n - k, n)
+            pltpu.make_async_remote_copy(
+                src_ref=src, dst_ref=buffer.at[source],
+                send_sem=sems.at[0, k], recv_sem=sems.at[1, k],
+                device_id=device(source), device_id_type=MESH,
+            ).wait_recv()
+        for copy in copies:
+            copy.wait_send()
+
+    def keep_stats():
+        parts[v] = stats_ref[...]
+
+    send_all(stats_ref, parts, v, n_voc, voc_sems, along_voc, keep_stats)
+    every = parts[...]
+    quarter = every.shape[1] // 4
+    peaks = every[:, :quarter]
+    peak = jnp.max(peaks, axis=0)
+    factor = jnp.exp(peaks - peak[None])
+    total = jnp.sum(every[:, quarter:2 * quarter] * factor, axis=0)
+    weighted = jnp.sum(every[:, 2 * quarter:3 * quarter] * factor, axis=0)
+    picked = jnp.sum(every[:, 3 * quarter:], axis=0)
+    log_total = peak + jnp.log(total)
+    live = live_ref[...] > 0.0
+    out_ref[g, :quarter] = jnp.where(live, picked - log_total, 0.0)
+    out_ref[g, quarter:] = jnp.where(live, log_total - weighted / total, 0.0)
+    send_all(out_ref.at[g], out_ref, g, n_grp, grp_sems, along_grp, lambda: None)
+
+
+def exchange(stats, live, n_voc, n_grp):
+    rows, lanes = stats.shape
+    return pl.pallas_call(
+        functools.partial(_exchange_kernel, n_voc, n_grp),
+        out_shape=jax.ShapeDtypeStruct((n_grp, rows // 2, lanes), stats.dtype),
+        in_specs=[pl.BlockSpec(memory_space=pltpu.VMEM)] * 2,
+        out_specs=pl.BlockSpec(memory_space=pltpu.VMEM),
+        scratch_shapes=[pltpu.VMEM((n_voc, rows, lanes), stats.dtype),
+                        pltpu.SemaphoreType.DMA((2, n_voc)), pltpu.SemaphoreType.DMA((2, n_grp))],
+        compiler_params=pltpu.CompilerParams(collective_id=0, has_side_effects=True),
+    )(stats, live)
 
 
 class _Ring:
@@ -245,17 +277,6 @@
     return full_rows, full_head.reshape(n_x * n_z * depth, vocab)
 
 
-def share(block, axis, other, n, collective_id):
-    return pl.pallas_call(
-        functools.partial(_share_kernel, axis, other, n),
-        out_shape=jax.ShapeDtypeStruct((n,) + block.shape, block.dtype),
-        in_specs=[pl.BlockSpec(memory_space=pltpu.VMEM)],
-        out_specs=pl.BlockSpec(memory_space=pltpu.VMEM),
-        scratch_shapes=[pltpu.SemaphoreType.DMA((n,)), pltpu.SemaphoreType.DMA((n,))],
-        compiler_params=pltpu.CompilerParams(collective_id=collective_id, has_side_effects=True),
-    )(block)
-
-
 def local(hidden, targets, row_count, norm_gain, head_weight, return_from, *, n_voc, n_grp, n_x, n_z):
     tok_rows = hidden.shape[0]
     positions = jnp.arange(tok_rows, dtype=jnp.int32)
@@ -271,18 +292,8 @@
     global_columns = lax.axis_index("voc") * vocab_local + jnp.arange(vocab_local, dtype=jnp.int32)
     picked = jnp.sum(jnp.where(global_columns[None, :] == targets[:, None], logits, 0.0), axis=1)
     stats = jnp.concatenate([peak, total, weighted, picked]).reshape(8, -1)
-    parts = share(stats, "voc", "grp", n_voc, 0).reshape(n_voc, 4, tok_rows)
-    peaks, totals, weights, picks = parts[:, 0], parts[:, 1], parts[:, 2], parts[:, 3]
-    peak_all = jnp.max(peaks, axis=0)
-    factor = jnp.exp(peaks - peak_all[None, :])
-    total_all = jnp.sum(totals * factor, axis=0)
-    weighted_all = jnp.sum(weights * factor, axis=0)
-    picked_all = jnp.sum(picks, axis=0)
-    log_total = peak_all + jnp.log(total_all)
-    logp = jnp.where(live_rows, picked_all - log_total, 0.0)
-    entropy = jnp.where(live_rows, log_total - weighted_all / total_all, 0.0)
-    both = jnp.concatenate([logp, entropy]).reshape(-1, 128)
-    results = share(both, "grp", "voc", n_grp, 1).reshape(n_grp, 2, tok_rows)
+    live = live_rows.astype(jnp.float32).reshape(2, -1)
+    results = exchange(stats, live, n_voc, n_grp).reshape(n_grp, 2, tok_rows)
     lanes = 128
     every = jnp.concatenate(
         [results[:, 0].reshape(-1, lanes), results[:, 1].reshape(-1, lanes)], axis=1)

time: 134 us -> 129 us (0.963)
  Pallas kernels: 109 us -> 105 us
    pallas_call x2 -> x1, Pallas kernels: 29.6 us -> 26.1 us  [exchange(): pl.pallas_call(functools.partial(_exchange_kernel, n_voc, n_grp), out_sha...]
where the time goes in v9:
time: 129 us
  Pallas kernels  105 us (81%)
  matrix products  11 us (9%)
  other arithmetic  7.49 us (6%)
  local copies, waits for them, and re-layouts  3.46 us (3%)
  between operations  1.41 us (1%)
    pallas_call x1, Pallas kernels, gather_both(): pl.pallas_call(functools.partial(_gather_kernel, n_x, n_z, n_y), out_shap...  79.1 us
    pallas_call x1, Pallas kernels, exchange(): pl.pallas_call(functools.partial(_exchange_kernel, n_voc, n_grp), out_sha...  26.1 us
    dot_general x1, matrix products, local(): logits = jnp.dot(normed, piece, preferred_element_type=jnp.float32)  10.3 us
    reduce_sum x1, other arithmetic, normalize(): jnp.mean(values * values, axis=1, keepdims=True) + EPSILON  4.22 us

profile of v9, /device:TPU:1, one launch (start us, length us, event | category | flops | bytes accessed | tf_op | source)
XLA Modules:
  0.0 128.5 jit_solution(5039899439515048977)
XLA Ops:
  0.6 0.0 copy-start.1
  0.6 1.8 %copy.8.head_ref = bf16[128,1000]{1,0:T(8,128)(2,1)} copy(bf16[128,1000]{0,1:T(8,128)(2,1)} %param.10) | data formatting | bytes 512000 | tf_op args[4]
  2.5 79.1 %shard_map.77 = (bf16[768,4096]{1,0:T(8,128)(2,1)}, bf16[4,8,128,1000]{3,2,1,0:T(8,128)(2,1)}) custom-call(bf16[768,256]{1,0:T(8,128)(2,1)} %rows_ref.1, bf16[128,1000]{1,0:T(8,128)(2,1)} %copy.8.head_ref), custom_call_target="tpu_custom_call" | custom-call | tf_op jit(solution)/shard_map/pallas_call | solution.py:267
  81.6 0.0 copy-start
  81.6 4.2 %fusion = f32[768]{0:T(1024)S(1)} fusion(bf16[768,4096]{1,0:T(8,128)(2,1)} %get-tuple-element.4), kind=kLoop, calls=%fused_computation.2 | loop fusion | flops 9436416 | bytes 6294528 | tf_op jit(solution)/shard_map/reduce_sum | solution.py:17
  85.8 0.0 copy-done.1
  85.8 0.3 copy-done
  86.2 0.0 copy-start.2
  86.2 0.0 copy-start.3
  86.2 10.3 %fusion.19 = (f32[768]{0:T(1024)S(1)}, f32[768,1000]{0,1:T(8,128)S(1)}) fusion(bf16[4096,1000]{1,0:T(8,128)(2,1)} %bitcast.8, bf16[768,4096]{1,0:T(8,128)(2,1)S(1)} %copy-done, f32[4096]{0:T(1024)S(1)} %convert_element_type.15, f32[768]{0:T(1024)S(1)} %add_rsqrt_fusion), kind=kOutput, calls=%fused_computation.37 | convolution fusion | flops 6304805888 | bytes 17577984 | tf_op jit(solution)/shard_map/dot_general | solution.py:287
  96.5 0.0 copy-done.2
  96.5 1.4 %fusion.7 = (f32[768]{0:T(1024)S(1)}, f32[768]{0:T(1024)S(1)}, f32[768]{0:T(1024)S(1)}) fusion(f32[768,1000]{0,1:T(8,128)S(1)} %get-tuple-element.16, f32[768]{0:T(1024)S(1)} %get-tuple-element.15, s32[768]{0:T(1024)S(1)} %copy-done.2, s32[1000]{0:T(1024)S(1)} %iota_add_fusion), kind=kLoop, calls=%fused_computation.11 | loop fusion | flops 5373696 | bytes 3091360 | tf_op jit(solution)/shard_map/reduce_sum | solution.py:290
  97.9 0.6 pad_maximum_fusion.stats_ref
  99.2 0.6 compare_convert_fusion.live_ref
  99.8 26.1 %shard_map.78 = f32[32,4,384]{2,1,0:T(4,128)} custom-call(f32[8,384]{1,0:T(8,128)} %pad_maximum_fusion.stats_ref, f32[2,384]{1,0:T(2,128)} %compare_convert_fusion.live_ref), custom_call_target="tpu_custom_call" | custom-call | tf_op jit(solution)/shard_map/pallas_call | solution.py:80
  125.9 1.1 reshape.35
  127.0 0.2 fusion.18
  127.1 0.0 copy-done.3
  127.1 0.7 fusion.8
  127.9 0.7 fusion.9
  (8 shorter events, 0.1 us)
Async XLA Ops:
  0.6 85.2 %copy-start.1 = (bf16[4096]{0:T(1024)(128)(2,1)S(1)}, bf16[4096]{0:T(1024)(128)(2,1)}, u32[]{:S(2)}) copy-start(bf16[4096]{0:T(1024)(128)(2,1)} %param.9) | copy-start | bytes 24580
  81.6 4.6 %copy-start = (bf16[768,4096]{1,0:T(8,128)(2,1)S(1)}, bf16[768,4096]{1,0:T(8,128)(2,1)}, u32[]{:S(2)}) copy-start(bf16[768,4096]{1,0:T(8,128)(2,1)} %get-tuple-element.4) | copy-start | bytes 18874372
  86.2 10.3 %copy-start.2 = (s32[768]{0:T(1024)S(1)}, s32[768]{0:T(1024)}, u32[]{:S(2)}) copy-start(s32[768]{0:T(1024)} %param.7) | copy-start | bytes 9220
  86.2 41.0 %copy-start.3 = (s32[768]{0:T(1024)S(1)}, s32[768]{0:T(1024)}, u32[]{:S(2)}) copy-start(s32[768]{0:T(1024)} %param.11) | copy-start | bytes 9220

commit v10 on v9

--- a/solution.py
+++ b/solution.py
@@ -10,12 +10,6 @@
 MESH = pl.DeviceIdType.MESH
 
 EPSILON = 1e-05
-
-
-def normalize(raw, norm_gain):
-    values = raw.astype(jnp.float32)
-    scale = lax.rsqrt(jnp.mean(values * values, axis=1, keepdims=True) + EPSILON)
-    return (values * scale * norm_gain.astype(jnp.float32)[None, :]).astype(jnp.bfloat16)
 
 
 def _exchange_kernel(n_voc, n_grp, stats_ref, live_ref, out_ref, parts, voc_sems, grp_sems):
@@ -154,7 +148,8 @@
             copy.wait_send()
 
 
-def _gather_kernel(n_x, n_z, n_y, rows_ref, head_ref, rows_out, head_out, local_sem, sems, pair_sems):
+def _gather_kernel(n_x, n_z, n_y, rows_ref, head_ref, gain_ref, normed_out, head_out, rows_out,
+                   local_sem, sems, pair_sems):
     me = lax.axis_index("grp")
     v = lax.axis_index("voc")
     x = me // n_z
@@ -243,8 +238,6 @@
     rows.finish_recv()
     second_x.advance()
     second_z.advance()
-    second_z.finish_recv()
-    second_x.finish_recv()
     for t in range(n_y):
         other = t * 2 + 1 - c
         block = rows_out.at[:, cols(other)]
@@ -253,27 +246,41 @@
             send_sem=pair_sems.at[0, t], recv_sem=pair_sems.at[1, t],
             device_id=(me, partner), device_id_type=MESH,
         ).wait_recv()
+    chunk = 64
+
+    def norm_chunk(i, carry):
+        start = pl.multiple_of(i * chunk, chunk)
+        values = rows_out[pl.ds(start, chunk), :].astype(jnp.float32)
+        scale = lax.rsqrt(jnp.mean(values * values, axis=1, keepdims=True) + EPSILON)
+        normed_out[pl.ds(start, chunk), :] = (values * scale * gain_ref[...]).astype(normed_out.dtype)
+        return carry
+
+    lax.fori_loop(0, rows_out.shape[0] // chunk, norm_chunk, 0)
+    second_z.finish_recv()
+    second_x.finish_recv()
     for ring in (first_x, first_z, second_z, second_x, rows):
         ring.finish_send()
     for copy in pair_copies:
         copy.wait_send()
 
 
-def gather_both(hidden, piece, n_x, n_z, n_voc):
+def gather_both(hidden, piece, norm_gain, n_x, n_z, n_voc):
     rows, width = hidden.shape
     depth, vocab = piece.shape
     n_y = n_voc // 2
     steps = max(n_x, n_z, n_y)
+    gain = norm_gain.astype(jnp.float32)[None, :]
     full_rows, full_head = pl.pallas_call(
         functools.partial(_gather_kernel, n_x, n_z, n_y),
         out_shape=(jax.ShapeDtypeStruct((rows, width * n_voc), hidden.dtype),
                    jax.ShapeDtypeStruct((n_x, n_z, depth, vocab), piece.dtype)),
-        in_specs=[pl.BlockSpec(memory_space=pltpu.VMEM)] * 2,
+        in_specs=[pl.BlockSpec(memory_space=pltpu.VMEM)] * 3,
         out_specs=(pl.BlockSpec(memory_space=pltpu.VMEM), pl.BlockSpec(memory_space=pltpu.VMEM)),
-        scratch_shapes=[pltpu.SemaphoreType.DMA((1,)), pltpu.SemaphoreType.DMA((5, 4, steps)),
+        scratch_shapes=[pltpu.VMEM((rows, width * n_voc), hidden.dtype),
+                        pltpu.SemaphoreType.DMA((1,)), pltpu.SemaphoreType.DMA((5, 4, steps)),
                         pltpu.SemaphoreType.DMA((2, n_y))],
         compiler_params=pltpu.CompilerParams(collective_id=3, has_side_effects=True),
-    )(hidden, piece)
+    )(hidden, piece, gain)
     return full_rows, full_head.reshape(n_x * n_z * depth, vocab)
 
 
@@ -281,8 +288,7 @@
     tok_rows = hidden.shape[0]
     positions = jnp.arange(tok_rows, dtype=jnp.int32)
     live_rows = positions < row_count[0]
-    full_rows, piece = gather_both(hidden, head_weight, n_x, n_z, n_voc)
-    normed = normalize(full_rows, norm_gain)
+    normed, piece = gather_both(hidden, head_weight, norm_gain, n_x, n_z, n_voc)
     vocab_local = head_weight.shape[1]
     logits = jnp.dot(normed, piece, preferred_element_type=jnp.float32)
     peak = jnp.max(logits, axis=1)

time: 129 us -> 126 us (0.977)
  other arithmetic: 7.49 us -> 4.55 us
    reduce_sum x1 -> x0, other arithmetic: 4.22 us -> none  [normalize(): jnp.mean(values * values, axis=1, keepdims=True) + EPSILON]
    broadcast_in_dim x0 -> x1, other arithmetic: none -> 1.3 us  [gather_both(): gain = norm_gain.astype(jnp.float32)[None, :]]
where the time goes in v10:
time: 126 us
  Pallas kernels  105 us (83%)
  matrix products  11.9 us (9%)
  other arithmetic  4.55 us (4%)
  local copies, waits for them, and re-layouts  3.13 us (2%)
  between operations  1.39 us (1%)
    pallas_call x1, Pallas kernels, gather_both(): pl.pallas_call(functools.partial(_gather_kernel, n_x, n_z, n_y), out_shap...  79.1 us
    pallas_call x1, Pallas kernels, exchange(): pl.pallas_call(functools.partial(_exchange_kernel, n_voc, n_grp), out_sha...  26.1 us
    dot_general x1, matrix products, local(): logits = jnp.dot(normed, piece, preferred_element_type=jnp.float32)  11.2 us

profile of v10, /device:TPU:1, one launch (start us, length us, event | category | flops | bytes accessed | tf_op | source)
XLA Modules:
  0.0 126.2 jit_solution(2705381155596537851)
XLA Ops:
  0.6 1.8 %copy.8.head_ref = bf16[128,1000]{1,0:T(8,128)(2,1)} copy(bf16[128,1000]{0,1:T(8,128)(2,1)} %param.10) | data formatting | bytes 512000 | tf_op args[4]
  2.5 1.3 %broadcast_in_dim.25 = f32[4096]{0:T(1024)} convert(bf16[4096]{0:T(1024)(128)(2,1)} %param.9) | non-fusion elementwise | flops 4096 | bytes 24576 | tf_op jit(solution)/shard_map/broadcast_in_dim | solution.py:272
  3.8 79.1 %shard_map.77 = (bf16[768,4096]{1,0:T(8,128)(2,1)}, bf16[4,8,128,1000]{3,2,1,0:T(8,128)(2,1)}) custom-call(bf16[768,256]{1,0:T(8,128)(2,1)} %rows_ref.1, bf16[128,1000]{1,0:T(8,128)(2,1)} %copy.8.head_ref, f32[1,4096]{1,0:T(1,128)} %bitcast.10), custom_call_target="tpu_custom_call" | custom-call | tf_op jit(solution)/shard_map/pallas_call | solution.py:273
  82.8 0.0 copy-start
  82.8 11.2 %fusion.12 = (f32[768]{0:T(1024)S(1)}, f32[768,1000]{0,1:T(8,128)S(1)}) fusion(bf16[768,4096]{1,0:T(8,128)(2,1)} %get-tuple-element.4, bf16[4096,1000]{1,0:T(8,128)(2,1)} %bitcast.11), kind=kOutput, calls=%fused_computation.28 | convolution fusion | flops 6292222976 | bytes 17558528 | tf_op jit(solution)/shard_map/dot_general | solution.py:293
  94.1 0.0 copy-start.1
  94.1 0.0 copy-done
  94.1 1.4 %fusion = (f32[768]{0:T(1024)S(1)}, f32[768]{0:T(1024)S(1)}, f32[768]{0:T(1024)S(1)}) fusion(f32[768,1000]{0,1:T(8,128)S(1)} %get-tuple-element.16, f32[768]{0:T(1024)S(1)} %get-tuple-element.15, s32[768]{0:T(1024)S(1)} %copy-done, s32[1000]{0:T(1024)S(1)} %iota_add_fusion), kind=kLoop, calls=%fused_computation.3 | loop fusion | flops 5373696 | bytes 3091360 | tf_op jit(solution)/shard_map/reduce_sum | solution.py:296
  95.6 0.6 pad_maximum_fusion.stats_ref
  96.8 0.6 compare_convert_fusion.live_ref
  97.4 26.1 %shard_map.78 = f32[32,4,384]{2,1,0:T(4,128)} custom-call(f32[8,384]{1,0:T(8,128)} %pad_maximum_fusion.stats_ref, f32[2,384]{1,0:T(2,128)} %compare_convert_fusion.live_ref), custom_call_target="tpu_custom_call" | custom-call | tf_op jit(solution)/shard_map/pallas_call | solution.py:74
  123.5 1.1 reshape.26
  124.6 0.2 fusion.11
  124.8 0.0 copy-done.1
  124.8 0.7 fusion.1
  125.5 0.7 fusion.2
  (6 shorter events, 0.1 us)
Async XLA Ops:
  82.8 11.3 %copy-start = (s32[768]{0:T(1024)S(1)}, s32[768]{0:T(1024)}, u32[]{:S(2)}) copy-start(s32[768]{0:T(1024)} %param.7) | copy-start | bytes 9220
  94.1 30.7 %copy-start.1 = (s32[768]{0:T(1024)S(1)}, s32[768]{0:T(1024)}, u32[]{:S(2)}) copy-start(s32[768]{0:T(1024)} %param.11) | copy-start | bytes 9220

commit v11 on v10

--- a/solution.py
+++ b/solution.py
@@ -252,7 +252,8 @@
         start = pl.multiple_of(i * chunk, chunk)
         values = rows_out[pl.ds(start, chunk), :].astype(jnp.float32)
         scale = lax.rsqrt(jnp.mean(values * values, axis=1, keepdims=True) + EPSILON)
-        normed_out[pl.ds(start, chunk), :] = (values * scale * gain_ref[...]).astype(normed_out.dtype)
+        gain = gain_ref[...].astype(jnp.float32)
+        normed_out[pl.ds(start, chunk), :] = (values * scale * gain).astype(normed_out.dtype)
         return carry
 
     lax.fori_loop(0, rows_out.shape[0] // chunk, norm_chunk, 0)
@@ -269,7 +270,7 @@
     depth, vocab = piece.shape
     n_y = n_voc // 2
     steps = max(n_x, n_z, n_y)
-    gain = norm_gain.astype(jnp.float32)[None, :]
+    gain = norm_gain.reshape(1, -1)
     full_rows, full_head = pl.pallas_call(
         functools.partial(_gather_kernel, n_x, n_z, n_y),
         out_shape=(jax.ShapeDtypeStruct((rows, width * n_voc), hidden.dtype),

time: 126 us -> 127 us (level)
  other arithmetic: 4.55 us -> 3.25 us
  local copies, waits for them, and re-layouts: 3.13 us -> 4.43 us
    reshape x0 -> x1, local copies, waits for them, and re-layouts: none -> 1.3 us  [gather_both(): gain = norm_gain.reshape(1, -1)]
    broadcast_in_dim x1 -> x0, other arithmetic: 1.3 us -> none  [gather_both(): gain = norm_gain.astype(jnp.float32)[None, :]]
where the time goes in v11:
time: 127 us; the launch traced here: 126 us
  Pallas kernels  105 us (83%)
  matrix products  11.9 us (9%)
  local copies, waits for them, and re-layouts  4.43 us (3%)
  other arithmetic  3.25 us (3%)
  between operations  1.39 us (1%)
    pallas_call x1, Pallas kernels, gather_both(): pl.pallas_call(functools.partial(_gather_kernel, n_x, n_z, n_y), out_shap...  79.1 us
    pallas_call x1, Pallas kernels, exchange(): pl.pallas_call(functools.partial(_exchange_kernel, n_voc, n_grp), out_sha...  26.1 us
    dot_general x1, matrix products, local(): logits = jnp.dot(normed, piece, preferred_element_type=jnp.float32)  11.2 us

profile of v11, /device:TPU:1, one launch (start us, length us, event | category | flops | bytes accessed | tf_op | source)
XLA Modules:
  0.0 126.2 jit_solution(12568183247652984183)
XLA Ops:
  0.6 1.8 %copy.8.head_ref = bf16[128,1000]{1,0:T(8,128)(2,1)} copy(bf16[128,1000]{0,1:T(8,128)(2,1)} %param.10) | data formatting | bytes 512000 | tf_op args[4]
  2.5 1.3 %reshape.28.gain_ref = bf16[1,4096]{1,0:T(2,128)(2,1)} reshape(bf16[4096]{0:T(1024)(128)(2,1)} %param.9) | data formatting | bytes 16384 | tf_op jit(solution)/shard_map/reshape | solution.py:273
  3.8 79.1 %shard_map.77 = (bf16[768,4096]{1,0:T(8,128)(2,1)}, bf16[4,8,128,1000]{3,2,1,0:T(8,128)(2,1)}) custom-call(bf16[768,256]{1,0:T(8,128)(2,1)} %rows_ref.1, bf16[128,1000]{1,0:T(8,128)(2,1)} %copy.8.head_ref, bf16[1,4096]{1,0:T(2,128)(2,1)} %reshape.28.gain_ref), custom_call_target="tpu_custom_call" | custom-call | tf_op jit(solution)/shard_map/pallas_call | solution.py:274
  82.8 0.0 copy-start
  82.8 11.2 %fusion.12 = (f32[768]{0:T(1024)S(1)}, f32[768,1000]{0,1:T(8,128)S(1)}) fusion(bf16[768,4096]{1,0:T(8,128)(2,1)} %get-tuple-element.4, bf16[4096,1000]{1,0:T(8,128)(2,1)} %bitcast.9), kind=kOutput, calls=%fused_computation.28 | convolution fusion | flops 6292222976 | bytes 17558528 | tf_op jit(solution)/shard_map/dot_general | solution.py:294
  94.1 0.0 copy-start.1
  94.1 0.0 copy-done
  94.1 1.4 %fusion = (f32[768]{0:T(1024)S(1)}, f32[768]{0:T(1024)S(1)}, f32[768]{0:T(1024)S(1)}) fusion(f32[768,1000]{0,1:T(8,128)S(1)} %get-tuple-element.16, f32[768]{0:T(1024)S(1)} %get-tuple-element.15, s32[768]{0:T(1024)S(1)} %copy-done, s32[1000]{0:T(1024)S(1)} %iota_add_fusion), kind=kLoop, calls=%fused_computation.3 | loop fusion | flops 5373696 | bytes 3091360 | tf_op jit(solution)/shard_map/reduce_sum | solution.py:297
  95.6 0.6 pad_maximum_fusion.stats_ref
  96.8 0.6 compare_convert_fusion.live_ref
  97.4 26.1 %shard_map.78 = f32[32,4,384]{2,1,0:T(4,128)} custom-call(f32[8,384]{1,0:T(8,128)} %pad_maximum_fusion.stats_ref, f32[2,384]{1,0:T(2,128)} %compare_convert_fusion.live_ref), custom_call_target="tpu_custom_call" | custom-call | tf_op jit(solution)/shard_map/pallas_call | solution.py:74
  123.5 1.1 reshape.30
  124.6 0.2 fusion.11
  124.8 0.0 copy-done.1
  124.8 0.7 fusion.1
  125.5 0.7 fusion.2
  (6 shorter events, 0.1 us)
Async XLA Ops:
  82.8 11.3 %copy-start = (s32[768]{0:T(1024)S(1)}, s32[768]{0:T(1024)}, u32[]{:S(2)}) copy-start(s32[768]{0:T(1024)} %param.7) | copy-start | bytes 9220
  94.1 30.7 %copy-start.1 = (s32[768]{0:T(1024)S(1)}, s32[768]{0:T(1024)}, u32[]{:S(2)}) copy-start(s32[768]{0:T(1024)} %param.11) | copy-start | bytes 9220

commit v12 on v10

--- a/solution.py
+++ b/solution.py
@@ -83,12 +83,13 @@
 
 
 class _Ring:
-    def __init__(self, pos, n, device, slot, own, sems, on_arrival=None):
+    def __init__(self, pos, n, device, slot, own, sems, on_arrival=None, split=True):
         self.pos, self.n, self.device, self.slot, self.own = pos, n, device, slot, own
         self.sems = sems
         self.on_arrival = on_arrival
-        self.steps = n // 2
-        self.split = n % 2 == 0
+        self.split = split and n % 2 == 0
+        self.counts = (n // 2, n // 2) if self.split else (n // 2, n - 1 - n // 2)
+        self.steps = max(self.counts)
         self.copies = []
         self.next = 1
 
@@ -113,7 +114,9 @@
     def step(self, s):
         if s > self.steps:
             return
-        for kind, sign in ((0, 1), (2, -1)):
+        for (kind, sign), count in zip(((0, 1), (2, -1)), self.counts):
+            if s > count:
+                continue
             target = self._origin(1, sign)
             origin = self._origin(s - 1, -sign)
             part = self._part(s, kind)
@@ -134,10 +137,12 @@
         if not self.steps:
             return
         last = []
-        for kind, sign in ((0, 1), (2, -1)):
-            origin = self._origin(self.steps, -sign)
-            view = self.slot(origin, self._part(self.steps, kind))
-            self._desc(view, origin, kind, self.steps, self._origin(1, sign)).wait_recv()
+        for (kind, sign), count in zip(((0, 1), (2, -1)), self.counts):
+            if not count:
+                continue
+            origin = self._origin(count, -sign)
+            view = self.slot(origin, self._part(count, kind))
+            self._desc(view, origin, kind, count, self._origin(1, sign)).wait_recv()
             last.append(origin)
         if self.on_arrival is not None:
             for origin in last[:1] if self.split else last:
@@ -157,8 +162,8 @@
     y = v // 2
     c = v % 2
     partner = y * 2 + 1 - c
-    half = head_ref.shape[0] // 2
-    lo, hi = pl.ds(0, half), pl.ds(half, half)
+    half = head_ref.shape[0] * 3 // 8
+    lo, hi = pl.ds(0, half), pl.ds(half, head_ref.shape[0] - half)
     width = rows_ref.shape[1]
 
     def cols(t):
@@ -206,14 +211,14 @@
         return lambda part: pl.ds(start, size) if part is None else pl.ds(start + part * (size // 2), size // 2)
 
     rows_part = halves(rows_ref.shape[0])
-    lo_part, hi_part = halves(half), halves(half, half)
+    lo_part, hi_part = halves(half), halves(head_ref.shape[0] - half, half)
     x_part, z_part = halves(n_x), halves(n_z)
     rows = _Ring(y, n_y, along_y, lambda t, p=None: rows_out.at[rows_part(p), cols(t * 2 + c)],
                  lambda p: rows_ref.at[rows_part(p)], sems.at[4], forward)
     first_x = _Ring(x, n_x, along_x, lambda t, p=None: head_out.at[t, z, lo_part(p)],
-                    lambda p: head_ref.at[lo_part(p)], sems.at[0])
+                    lambda p: head_ref.at[lo_part(p)], sems.at[0], split=False)
     first_z = _Ring(z, n_z, along_z, lambda t, p=None: head_out.at[x, t, hi_part(p)],
-                    lambda p: head_ref.at[hi_part(p)], sems.at[1])
+                    lambda p: head_ref.at[hi_part(p)], sems.at[1], split=False)
     rows.advance()
     first_x.advance()
     first_z.advance()

time: 126 us -> 132 us (1.048)
  Pallas kernels: 105 us -> 111 us
    pallas_call x1, Pallas kernels: 79.1 us -> 84.7 us  [gather_both(): pl.pallas_call(functools.partial(_gather_kernel, n_x, n_z, n_y), out_shap...]
where the time goes in v12:
time: 132 us
  Pallas kernels  111 us (84%)
  matrix products  12 us (9%)
  other arithmetic  4.55 us (3%)
  local copies, waits for them, and re-layouts  3.13 us (2%)
  between operations  1.39 us (1%)
    pallas_call x1, Pallas kernels, gather_both(): pl.pallas_call(functools.partial(_gather_kernel, n_x, n_z, n_y), out_shap...  84.7 us
    pallas_call x1, Pallas kernels, exchange(): pl.pallas_call(functools.partial(_exchange_kernel, n_voc, n_grp), out_sha...  25.8 us
    dot_general x1, matrix products, local(): logits = jnp.dot(normed, piece, preferred_element_type=jnp.float32)  11.2 us

profile of v12, /device:TPU:1, one launch (start us, length us, event | category | flops | bytes accessed | tf_op | source)
XLA Modules:
  0.0 131.6 jit_solution(16736429490066932976)
XLA Ops:
  0.6 1.8 %copy.8.head_ref = bf16[128,1000]{1,0:T(8,128)(2,1)} copy(bf16[128,1000]{0,1:T(8,128)(2,1)} %param.10) | data formatting | bytes 512000 | tf_op args[4]
  2.5 1.3 broadcast_in_dim.25
  3.8 84.7 %shard_map.77 = (bf16[768,4096]{1,0:T(8,128)(2,1)}, bf16[4,8,128,1000]{3,2,1,0:T(8,128)(2,1)}) custom-call(bf16[768,256]{1,0:T(8,128)(2,1)} %rows_ref.1, bf16[128,1000]{1,0:T(8,128)(2,1)} %copy.8.head_ref, f32[1,4096]{1,0:T(1,128)} %bitcast.10), custom_call_target="tpu_custom_call" | custom-call | tf_op jit(solution)/shard_map/pallas_call | solution.py:278
  88.5 0.0 copy-start
  88.5 11.2 %fusion.12 = (f32[768]{0:T(1024)S(1)}, f32[768,1000]{0,1:T(8,128)S(1)}) fusion(bf16[768,4096]{1,0:T(8,128)(2,1)} %get-tuple-element.4, bf16[4096,1000]{1,0:T(8,128)(2,1)} %bitcast.11), kind=kOutput, calls=%fused_computation.28 | convolution fusion | flops 6292222976 | bytes 17558528 | tf_op jit(solution)/shard_map/dot_general | solution.py:298
  99.8 0.0 copy-start.1
  99.8 0.0 copy-done
  99.8 1.4 %fusion = (f32[768]{0:T(1024)S(1)}, f32[768]{0:T(1024)S(1)}, f32[768]{0:T(1024)S(1)}) fusion(f32[768,1000]{0,1:T(8,128)S(1)} %get-tuple-element.16, f32[768]{0:T(1024)S(1)} %get-tuple-element.15, s32[768]{0:T(1024)S(1)} %copy-done, s32[1000]{0:T(1024)S(1)} %iota_add_fusion), kind=kLoop, calls=%fused_computation.3 | loop fusion | flops 5373696 | bytes 3091360 | tf_op jit(solution)/shard_map/reduce_sum | solution.py:301
  101.2 0.6 pad_maximum_fusion.stats_ref
  102.5 0.6 compare_convert_fusion.live_ref
  103.1 25.8 %shard_map.78 = f32[32,4,384]{2,1,0:T(4,128)} custom-call(f32[8,384]{1,0:T(8,128)} %pad_maximum_fusion.stats_ref, f32[2,384]{1,0:T(2,128)} %compare_convert_fusion.live_ref), custom_call_target="tpu_custom_call" | custom-call | tf_op jit(solution)/shard_map/pallas_call | solution.py:74
  128.9 1.1 reshape.26
  130.0 0.2 fusion.11
  130.2 0.0 copy-done.1
  130.2 0.7 fusion.1
  130.9 0.7 fusion.2
  (6 shorter events, 0.1 us)
Async XLA Ops:
  88.5 11.3 %copy-start = (s32[768]{0:T(1024)S(1)}, s32[768]{0:T(1024)}, u32[]{:S(2)}) copy-start(s32[768]{0:T(1024)} %param.7) | copy-start | bytes 9220
  99.8 30.4 %copy-start.1 = (s32[768]{0:T(1024)S(1)}, s32[768]{0:T(1024)}, u32[]{:S(2)}) copy-start(s32[768]{0:T(1024)} %param.11) | copy-start | bytes 9220

commit v13 on v10

--- a/solution.py
+++ b/solution.py
@@ -12,7 +12,7 @@
 EPSILON = 1e-05
 
 
-def _exchange_kernel(n_voc, n_grp, stats_ref, live_ref, out_ref, parts, voc_sems, grp_sems):
+def _exchange_kernel(n_voc, n_grp, stats_ref, count_ref, out_ref, parts, voc_sems, grp_sems):
     g = lax.axis_index("grp")
     v = lax.axis_index("voc")
 
@@ -63,13 +63,15 @@
     weighted = jnp.sum(every[:, 2 * quarter:3 * quarter] * factor, axis=0)
     picked = jnp.sum(every[:, 3 * quarter:], axis=0)
     log_total = peak + jnp.log(total)
-    live = live_ref[...] > 0.0
+    shape = peak.shape
+    row = lax.broadcasted_iota(jnp.int32, shape, 0) * shape[1] + lax.broadcasted_iota(jnp.int32, shape, 1)
+    live = row < count_ref[...]
     out_ref[g, :quarter] = jnp.where(live, picked - log_total, 0.0)
     out_ref[g, quarter:] = jnp.where(live, log_total - weighted / total, 0.0)
     send_all(out_ref.at[g], out_ref, g, n_grp, grp_sems, along_grp, lambda: None)
 
 
-def exchange(stats, live, n_voc, n_grp):
+def exchange(stats, count, n_voc, n_grp):
     rows, lanes = stats.shape
     return pl.pallas_call(
         functools.partial(_exchange_kernel, n_voc, n_grp),
@@ -79,7 +81,7 @@
         scratch_shapes=[pltpu.VMEM((n_voc, rows, lanes), stats.dtype),
                         pltpu.SemaphoreType.DMA((2, n_voc)), pltpu.SemaphoreType.DMA((2, n_grp))],
         compiler_params=pltpu.CompilerParams(collective_id=0, has_side_effects=True),
-    )(stats, live)
+    )(stats, count)
 
 
 class _Ring:
@@ -286,8 +288,6 @@
 
 def local(hidden, targets, row_count, norm_gain, head_weight, return_from, *, n_voc, n_grp, n_x, n_z):
     tok_rows = hidden.shape[0]
-    positions = jnp.arange(tok_rows, dtype=jnp.int32)
-    live_rows = positions < row_count[0]
     normed, piece = gather_both(hidden, head_weight, norm_gain, n_x, n_z, n_voc)
     vocab_local = head_weight.shape[1]
     logits = jnp.dot(normed, piece, preferred_element_type=jnp.float32)
@@ -298,8 +298,7 @@
     global_columns = lax.axis_index("voc") * vocab_local + jnp.arange(vocab_local, dtype=jnp.int32)
     picked = jnp.sum(jnp.where(global_columns[None, :] == targets[:, None], logits, 0.0), axis=1)
     stats = jnp.concatenate([peak, total, weighted, picked]).reshape(8, -1)
-    live = live_rows.astype(jnp.float32).reshape(2, -1)
-    results = exchange(stats, live, n_voc, n_grp).reshape(n_grp, 2, tok_rows)
+    results = exchange(stats, row_count.reshape(1, 1), n_voc, n_grp).reshape(n_grp, 2, tok_rows)
     lanes = 128
     every = jnp.concatenate(
         [results[:, 0].reshape(-1, lanes), results[:, 1].reshape(-1, lanes)], axis=1)

time: 126 us -> 126 us (level)
  no operation moved by 1% of the time
where the time goes in v13:
time: 126 us
  Pallas kernels  105 us (83%)
  matrix products  11.9 us (9%)
  other arithmetic  3.97 us (3%)
  local copies, waits for them, and re-layouts  3.13 us (2%)
  between operations  1.39 us (1%)
    pallas_call x1, Pallas kernels, gather_both(): pl.pallas_call(functools.partial(_gather_kernel, n_x, n_z, n_y), out_shap...  79.1 us
    pallas_call x1, Pallas kernels, exchange(): pl.pallas_call(functools.partial(_exchange_kernel, n_voc, n_grp), out_sha...  26.1 us
    dot_general x1, matrix products, local(): logits = jnp.dot(normed, piece, preferred_element_type=jnp.float32)  11.3 us

profile of v13, /device:TPU:1, one launch (start us, length us, event | category | flops | bytes accessed | tf_op | source)
XLA Modules:
  0.0 125.6 jit_solution(13825727085664048805)
XLA Ops:
  0.6 1.8 %copy.8.head_ref = bf16[128,1000]{1,0:T(8,128)(2,1)} copy(bf16[128,1000]{0,1:T(8,128)(2,1)} %param.10) | data formatting | bytes 512000 | tf_op args[4]
  2.5 1.3 %broadcast_in_dim.25 = f32[4096]{0:T(1024)} convert(bf16[4096]{0:T(1024)(128)(2,1)} %param.9) | non-fusion elementwise | flops 4096 | bytes 24576 | tf_op jit(solution)/shard_map/broadcast_in_dim | solution.py:274
  3.8 79.1 %shard_map.77 = (bf16[768,4096]{1,0:T(8,128)(2,1)}, bf16[4,8,128,1000]{3,2,1,0:T(8,128)(2,1)}) custom-call(bf16[768,256]{1,0:T(8,128)(2,1)} %rows_ref.1, bf16[128,1000]{1,0:T(8,128)(2,1)} %copy.8.head_ref, f32[1,4096]{1,0:T(1,128)} %bitcast.10), custom_call_target="tpu_custom_call" | custom-call | tf_op jit(solution)/shard_map/pallas_call | solution.py:275
  82.8 0.0 copy-start
  82.8 11.3 %fusion.12 = (f32[768]{0:T(1024)S(1)}, f32[768,1000]{0,1:T(8,128)S(1)}) fusion(bf16[768,4096]{1,0:T(8,128)(2,1)} %get-tuple-element.4, bf16[4096,1000]{1,0:T(8,128)(2,1)} %bitcast.11), kind=kOutput, calls=%fused_computation.27 | convolution fusion | flops 6292222976 | bytes 17558528 | tf_op jit(solution)/shard_map/dot_general | solution.py:293
  94.1 0.0 copy-start.1
  94.1 0.0 copy-done
  94.1 1.4 %fusion = (f32[768]{0:T(1024)S(1)}, f32[768]{0:T(1024)S(1)}, f32[768]{0:T(1024)S(1)}) fusion(f32[768,1000]{0,1:T(8,128)S(1)} %get-tuple-element.16, f32[768]{0:T(1024)S(1)} %get-tuple-element.15, s32[768]{0:T(1024)S(1)} %copy-done, s32[1000]{0:T(1024)S(1)} %iota_add_fusion), kind=kLoop, calls=%fused_computation.3 | loop fusion | flops 5373696 | bytes 3091360 | tf_op jit(solution)/shard_map/reduce_sum | solution.py:296
  95.6 0.6 pad_maximum_fusion.stats_ref
  96.8 26.1 %shard_map.78 = f32[32,4,384]{2,1,0:T(4,128)} custom-call(f32[8,384]{1,0:T(8,128)} %pad_maximum_fusion.stats_ref, s32[1,1]{1,0:T(1,128)} %bitcast.7.count_ref), custom_call_target="tpu_custom_call" | custom-call | tf_op jit(solution)/shard_map/pallas_call | solution.py:76
  123.0 1.1 reshape.28
  124.1 0.2 fusion.11
  124.2 0.0 copy-done.1
  124.2 0.7 fusion.1
  124.9 0.7 fusion.2
  (6 shorter events, 0.1 us)
Async XLA Ops:
  82.8 11.3 %copy-start = (s32[768]{0:T(1024)S(1)}, s32[768]{0:T(1024)}, u32[]{:S(2)}) copy-start(s32[768]{0:T(1024)} %param.7) | copy-start | bytes 9220
  94.1 30.1 %copy-start.1 = (s32[768]{0:T(1024)S(1)}, s32[768]{0:T(1024)}, u32[]{:S(2)}) copy-start(s32[768]{0:T(1024)} %param.11) | copy-start | bytes 9220

commit v14 on v13

--- a/solution.py
+++ b/solution.py
@@ -297,7 +297,7 @@
     weighted = jnp.sum(shifted * logits, axis=1)
     global_columns = lax.axis_index("voc") * vocab_local + jnp.arange(vocab_local, dtype=jnp.int32)
     picked = jnp.sum(jnp.where(global_columns[None, :] == targets[:, None], logits, 0.0), axis=1)
-    stats = jnp.concatenate([peak, total, weighted, picked]).reshape(8, -1)
+    stats = jnp.stack([peak, total, weighted, picked])
     results = exchange(stats, row_count.reshape(1, 1), n_voc, n_grp).reshape(n_grp, 2, tok_rows)
     lanes = 128
     every = jnp.concatenate(

time: 126 us -> 126 us (level)
  no operation moved by 1% of the time
where the time goes in v14:
time: 126 us
  Pallas kernels  105 us (83%)
  matrix products  12 us (10%)
  other arithmetic  3.97 us (3%)
  local copies, waits for them, and re-layouts  3.05 us (2%)
  between operations  1.41 us (1%)
    pallas_call x1, Pallas kernels, gather_both(): pl.pallas_call(functools.partial(_gather_kernel, n_x, n_z, n_y), out_shap...  79.1 us
    pallas_call x1, Pallas kernels, exchange(): pl.pallas_call(functools.partial(_exchange_kernel, n_voc, n_grp), out_sha...  26.2 us
    dot_general x1, matrix products, local(): logits = jnp.dot(normed, piece, preferred_element_type=jnp.float32)  11.3 us

profile of v14, /device:TPU:1, one launch (start us, length us, event | category | flops | bytes accessed | tf_op | source)
XLA Modules:
  0.0 125.7 jit_solution(13798005612426786700)
XLA Ops:
  0.6 1.8 %copy.8.head_ref = bf16[128,1000]{1,0:T(8,128)(2,1)} copy(bf16[128,1000]{0,1:T(8,128)(2,1)} %param.10) | data formatting | bytes 512000 | tf_op args[4]
  2.5 1.3 %broadcast_in_dim.25 = f32[4096]{0:T(1024)} convert(bf16[4096]{0:T(1024)(128)(2,1)} %param.9) | non-fusion elementwise | flops 4096 | bytes 24576 | tf_op jit(solution)/shard_map/broadcast_in_dim | solution.py:274
  3.8 79.1 %shard_map.77 = (bf16[768,4096]{1,0:T(8,128)(2,1)}, bf16[4,8,128,1000]{3,2,1,0:T(8,128)(2,1)}) custom-call(bf16[768,256]{1,0:T(8,128)(2,1)} %rows_ref.1, bf16[128,1000]{1,0:T(8,128)(2,1)} %copy.8.head_ref, f32[1,4096]{1,0:T(1,128)} %bitcast.10), custom_call_target="tpu_custom_call" | custom-call | tf_op jit(solution)/shard_map/pallas_call | solution.py:275
  82.8 0.0 copy-start
  82.8 11.3 %fusion.12 = (f32[768]{0:T(1024)S(1)}, f32[768,1000]{0,1:T(8,128)S(1)}) fusion(bf16[768,4096]{1,0:T(8,128)(2,1)} %get-tuple-element.4, bf16[4096,1000]{1,0:T(8,128)(2,1)} %bitcast.11), kind=kOutput, calls=%fused_computation.27 | convolution fusion | flops 6292222976 | bytes 17558528 | tf_op jit(solution)/shard_map/dot_general | solution.py:293
  94.1 0.0 copy-start.1
  94.1 0.0 copy-done
  94.1 1.4 %fusion = (f32[768]{0:T(1024)S(1)}, f32[768]{0:T(1024)S(1)}, f32[768]{0:T(1024)S(1)}) fusion(f32[768,1000]{0,1:T(8,128)S(1)} %get-tuple-element.16, f32[768]{0:T(1024)S(1)} %get-tuple-element.15, s32[768]{0:T(1024)S(1)} %copy-done, s32[1000]{0:T(1024)S(1)} %iota_add_fusion), kind=kLoop, calls=%fused_computation.3 | loop fusion | flops 5373696 | bytes 3091360 | tf_op jit(solution)/shard_map/reduce_sum | solution.py:296
  95.6 0.6 pad_maximum_fusion.stats_ref
  96.8 26.2 %shard_map.78 = f32[32,2,768]{2,1,0:T(2,128)} custom-call(f32[4,768]{1,0:T(4,128)} %pad_maximum_fusion.stats_ref, s32[1,1]{1,0:T(1,128)} %bitcast.7.count_ref), custom_call_target="tpu_custom_call" | custom-call | tf_op jit(solution)/shard_map/pallas_call | solution.py:76
  123.0 1.2 fusion.11
  124.2 0.0 copy-done.1
  124.3 0.7 fusion.1
  125.0 0.7 fusion.2
  (6 shorter events, 0.0 us)
Async XLA Ops:
  82.8 11.3 %copy-start = (s32[768]{0:T(1024)S(1)}, s32[768]{0:T(1024)}, u32[]{:S(2)}) copy-start(s32[768]{0:T(1024)} %param.7) | copy-start | bytes 9220
  94.1 30.1 %copy-start.1 = (s32[768]{0:T(1024)S(1)}, s32[768]{0:T(1024)}, u32[]{:S(2)}) copy-start(s32[768]{0:T(1024)} %param.11) | copy-start | bytes 9220

commit v15 on v12

--- a/solution.py
+++ b/solution.py
@@ -12,7 +12,7 @@
 EPSILON = 1e-05
 
 
-def _exchange_kernel(n_voc, n_grp, stats_ref, live_ref, out_ref, parts, voc_sems, grp_sems):
+def _exchange_kernel(n_voc, n_grp, stats_ref, count_ref, out_ref, parts, voc_sems, grp_sems):
     g = lax.axis_index("grp")
     v = lax.axis_index("voc")
 
@@ -63,13 +63,15 @@
     weighted = jnp.sum(every[:, 2 * quarter:3 * quarter] * factor, axis=0)
     picked = jnp.sum(every[:, 3 * quarter:], axis=0)
     log_total = peak + jnp.log(total)
-    live = live_ref[...] > 0.0
+    shape = peak.shape
+    row = lax.broadcasted_iota(jnp.int32, shape, 0) * shape[1] + lax.broadcasted_iota(jnp.int32, shape, 1)
+    live = row < count_ref[...]
     out_ref[g, :quarter] = jnp.where(live, picked - log_total, 0.0)
     out_ref[g, quarter:] = jnp.where(live, log_total - weighted / total, 0.0)
     send_all(out_ref.at[g], out_ref, g, n_grp, grp_sems, along_grp, lambda: None)
 
 
-def exchange(stats, live, n_voc, n_grp):
+def exchange(stats, count, n_voc, n_grp):
     rows, lanes = stats.shape
     return pl.pallas_call(
         functools.partial(_exchange_kernel, n_voc, n_grp),
@@ -79,7 +81,7 @@
         scratch_shapes=[pltpu.VMEM((n_voc, rows, lanes), stats.dtype),
                         pltpu.SemaphoreType.DMA((2, n_voc)), pltpu.SemaphoreType.DMA((2, n_grp))],
         compiler_params=pltpu.CompilerParams(collective_id=0, has_side_effects=True),
-    )(stats, live)
+    )(stats, count)
 
 
 class _Ring:
@@ -162,7 +164,7 @@
     y = v // 2
     c = v % 2
     partner = y * 2 + 1 - c
-    half = head_ref.shape[0] * 3 // 8
+    half = head_ref.shape[0] * 5 // 8
     lo, hi = pl.ds(0, half), pl.ds(half, head_ref.shape[0] - half)
     width = rows_ref.shape[1]
 
@@ -291,8 +293,6 @@
 
 def local(hidden, targets, row_count, norm_gain, head_weight, return_from, *, n_voc, n_grp, n_x, n_z):
     tok_rows = hidden.shape[0]
-    positions = jnp.arange(tok_rows, dtype=jnp.int32)
-    live_rows = positions < row_count[0]
     normed, piece = gather_both(hidden, head_weight, norm_gain, n_x, n_z, n_voc)
     vocab_local = head_weight.shape[1]
     logits = jnp.dot(normed, piece, preferred_element_type=jnp.float32)
@@ -302,9 +302,8 @@
     weighted = jnp.sum(shifted * logits, axis=1)
     global_columns = lax.axis_index("voc") * vocab_local + jnp.arange(vocab_local, dtype=jnp.int32)
     picked = jnp.sum(jnp.where(global_columns[None, :] == targets[:, None], logits, 0.0), axis=1)
-    stats = jnp.concatenate([peak, total, weighted, picked]).reshape(8, -1)
-    live = live_rows.astype(jnp.float32).reshape(2, -1)
-    results = exchange(stats, live, n_voc, n_grp).reshape(n_grp, 2, tok_rows)
+    stats = jnp.stack([peak, total, weighted, picked])
+    results = exchange(stats, row_count.reshape(1, 1), n_voc, n_grp).reshape(n_grp, 2, tok_rows)
     lanes = 128
     every = jnp.concatenate(
         [results[:, 0].reshape(-1, lanes), results[:, 1].reshape(-1, lanes)], axis=1)

time: 132 us -> 131 us (level)
    pallas_call x1, Pallas kernels: 84.7 us -> 83.1 us  [gather_both(): pl.pallas_call(functools.partial(_gather_kernel, n_x, n_z, n_y), out_shap...]
    pallas_call x1, Pallas kernels: 25.8 us -> 27.2 us  [exchange(): pl.pallas_call(functools.partial(_exchange_kernel, n_voc, n_grp), out_sha...]
where the time goes in v15:
time: 131 us
  Pallas kernels  110 us (84%)
  matrix products  12 us (9%)
  other arithmetic  3.97 us (3%)
  local copies, waits for them, and re-layouts  3.05 us (2%)
  between operations  1.41 us (1%)
    pallas_call x1, Pallas kernels, gather_both(): pl.pallas_call(functools.partial(_gather_kernel, n_x, n_z, n_y), out_shap...  83.1 us
    pallas_call x1, Pallas kernels, exchange(): pl.pallas_call(functools.partial(_exchange_kernel, n_voc, n_grp), out_sha...  27.2 us
    dot_general x1, matrix products, local(): logits = jnp.dot(normed, piece, preferred_element_type=jnp.float32)  11.2 us

profile of v15, /device:TPU:1, one launch (start us, length us, event | category | flops | bytes accessed | tf_op | source)
XLA Modules:
  0.0 130.7 jit_solution(17717306533167213583)
XLA Ops:
  0.6 1.8 %copy.8.head_ref = bf16[128,1000]{1,0:T(8,128)(2,1)} copy(bf16[128,1000]{0,1:T(8,128)(2,1)} %param.10) | data formatting | bytes 512000 | tf_op args[4]
  2.5 1.3 broadcast_in_dim.25
  3.8 83.1 %shard_map.77 = (bf16[768,4096]{1,0:T(8,128)(2,1)}, bf16[4,8,128,1000]{3,2,1,0:T(8,128)(2,1)}) custom-call(bf16[768,256]{1,0:T(8,128)(2,1)} %rows_ref.1, bf16[128,1000]{1,0:T(8,128)(2,1)} %copy.8.head_ref, f32[1,4096]{1,0:T(1,128)} %bitcast.10), custom_call_target="tpu_custom_call" | custom-call | tf_op jit(solution)/shard_map/pallas_call | solution.py:280
  86.8 0.0 copy-start
  86.9 11.2 %fusion.12 = (f32[768]{0:T(1024)S(1)}, f32[768,1000]{0,1:T(8,128)S(1)}) fusion(bf16[768,4096]{1,0:T(8,128)(2,1)} %get-tuple-element.4, bf16[4096,1000]{1,0:T(8,128)(2,1)} %bitcast.11), kind=kOutput, calls=%fused_computation.27 | convolution fusion | flops 6292222976 | bytes 17558528 | tf_op jit(solution)/shard_map/dot_general | solution.py:298
  98.1 0.0 copy-start.1
  98.1 0.0 copy-done
  98.2 1.4 %fusion = (f32[768]{0:T(1024)S(1)}, f32[768]{0:T(1024)S(1)}, f32[768]{0:T(1024)S(1)}) fusion(f32[768,1000]{0,1:T(8,128)S(1)} %get-tuple-element.16, f32[768]{0:T(1024)S(1)} %get-tuple-element.15, s32[768]{0:T(1024)S(1)} %copy-done, s32[1000]{0:T(1024)S(1)} %iota_add_fusion), kind=kLoop, calls=%fused_computation.3 | loop fusion | flops 5373696 | bytes 3091360 | tf_op jit(solution)/shard_map/reduce_sum | solution.py:301
  99.6 0.6 pad_maximum_fusion.stats_ref
  100.8 27.2 %shard_map.78 = f32[32,2,768]{2,1,0:T(2,128)} custom-call(f32[4,768]{1,0:T(4,128)} %pad_maximum_fusion.stats_ref, s32[1,1]{1,0:T(1,128)} %bitcast.7.count_ref), custom_call_target="tpu_custom_call" | custom-call | tf_op jit(solution)/shard_map/pallas_call | solution.py:76
  128.0 1.2 fusion.11
  129.2 0.0 copy-done.1
  129.3 0.7 fusion.1
  130.0 0.7 fusion.2
  (6 shorter events, 0.0 us)
Async XLA Ops:
  86.8 11.3 %copy-start = (s32[768]{0:T(1024)S(1)}, s32[768]{0:T(1024)}, u32[]{:S(2)}) copy-start(s32[768]{0:T(1024)} %param.7) | copy-start | bytes 9220
  98.1 31.1 %copy-start.1 = (s32[768]{0:T(1024)S(1)}, s32[768]{0:T(1024)}, u32[]{:S(2)}) copy-start(s32[768]{0:T(1024)} %param.11) | copy-start | bytes 9220

commit v16 on v14

--- a/solution.py
+++ b/solution.py
@@ -150,6 +150,38 @@
             copy.wait_send()
 
 
+class _Direct:
+    def __init__(self, pos, n, device, slot, own, sems):
+        self.pos, self.n, self.device, self.slot, self.own = pos, n, device, slot, own
+        self.sems = sems
+        self.copies = []
+
+    def _desc(self, src, origin, k, target):
+        return pltpu.make_async_remote_copy(
+            src_ref=src, dst_ref=self.slot(origin),
+            send_sem=self.sems.at[0, k - 1], recv_sem=self.sems.at[1, k - 1],
+            device_id=self.device(target), device_id_type=MESH,
+        )
+
+    def advance(self):
+        if self.copies:
+            return
+        for k in range(1, self.n):
+            copy = self._desc(self.own(None), self.pos, k, lax.rem(self.pos + k, self.n))
+            copy.start()
+            self.copies.append(copy)
+
+    def finish_recv(self):
+        self.advance()
+        for k in range(1, self.n):
+            origin = lax.rem(self.pos + self.n - k, self.n)
+            self._desc(self.slot(origin), origin, k, origin).wait_recv()
+
+    def finish_send(self):
+        for copy in self.copies:
+            copy.wait_send()
+
+
 def _gather_kernel(n_x, n_z, n_y, rows_ref, head_ref, gain_ref, normed_out, head_out, rows_out,
                    local_sem, sems, pair_sems):
     me = lax.axis_index("grp")
@@ -176,10 +208,9 @@
         return (me, t * 2 + c)
 
     barrier = pltpu.get_barrier_semaphore()
-    neighbours = [along_x(lax.rem(x + 1, n_x)), along_x(lax.rem(x + n_x - 1, n_x)),
-                  along_z(lax.rem(z + 1, n_z)), along_z(lax.rem(z + n_z - 1, n_z)),
-                  along_y(lax.rem(y + 1, n_y)), along_y(lax.rem(y + n_y - 1, n_y)),
-                  (me, partner)]
+    neighbours = ([along_x(lax.rem(x + k, n_x)) for k in range(1, n_x)]
+                  + [along_z(lax.rem(z + k, n_z)) for k in range(1, n_z)]
+                  + [along_y(lax.rem(y + 1, n_y)), along_y(lax.rem(y + n_y - 1, n_y)), (me, partner)])
     for target in neighbours:
         pl.semaphore_signal(barrier, inc=1, device_id=target, device_id_type=MESH)
     pl.semaphore_wait(barrier, len(neighbours))
@@ -208,17 +239,14 @@
         return lambda part: pl.ds(start, size) if part is None else pl.ds(start + part * (size // 2), size // 2)
 
     rows_part = halves(rows_ref.shape[0])
-    lo_part, hi_part = halves(half), halves(half, half)
     x_part, z_part = halves(n_x), halves(n_z)
     rows = _Ring(y, n_y, along_y, lambda t, p=None: rows_out.at[rows_part(p), cols(t * 2 + c)],
                  lambda p: rows_ref.at[rows_part(p)], sems.at[4], forward)
-    first_x = _Ring(x, n_x, along_x, lambda t, p=None: head_out.at[t, z, lo_part(p)],
-                    lambda p: head_ref.at[lo_part(p)], sems.at[0])
-    first_z = _Ring(z, n_z, along_z, lambda t, p=None: head_out.at[x, t, hi_part(p)],
-                    lambda p: head_ref.at[hi_part(p)], sems.at[1])
+    first_x = _Direct(x, n_x, along_x, lambda t: head_out.at[t, z, lo],
+                      lambda p: head_ref.at[lo], sems.at[0])
+    first_z = _Direct(z, n_z, along_z, lambda t: head_out.at[x, t, hi],
+                      lambda p: head_ref.at[hi], sems.at[1])
     rows.advance()
-    first_x.advance()
-    first_z.advance()
     first_x.advance()
     first_z.advance()
     own.wait()
@@ -228,9 +256,6 @@
     second_x = _Ring(x, n_x, along_x, lambda t, p=None: head_out.at[t, z_part(p), hi],
                      lambda p: head_out.at[x, z_part(p), hi], sems.at[3])
     second_z.advance()
-    first_z.advance()
-    rows.advance()
-    first_z.advance()
     first_z.finish_recv()
     second_x.advance()
     rows.advance()

time: 126 us -> 133 us (1.056)
  Pallas kernels: 105 us -> 112 us
    pallas_call x1, Pallas kernels: 79.1 us -> 84.1 us  [gather_both(): pl.pallas_call(functools.partial(_gather_kernel, n_x, n_z, n_y), out_shap...]
    pallas_call x1, Pallas kernels: 26.2 us -> 27.9 us  [exchange(): pl.pallas_call(functools.partial(_exchange_kernel, n_voc, n_grp), out_sha...]
where the time goes in v16:
time: 133 us; the launch traced here: 132 us
  Pallas kernels  112 us (84%)
  matrix products  12 us (9%)
  other arithmetic  3.97 us (3%)
  local copies, waits for them, and re-layouts  3.05 us (2%)
  between operations  1.41 us (1%)
    pallas_call x1, Pallas kernels, gather_both(): pl.pallas_call(functools.partial(_gather_kernel, n_x, n_z, n_y), out_shap...  84.1 us
    pallas_call x1, Pallas kernels, exchange(): pl.pallas_call(functools.partial(_exchange_kernel, n_voc, n_grp), out_sha...  27.9 us
    dot_general x1, matrix products, local(): logits = jnp.dot(normed, piece, preferred_element_type=jnp.float32)  11.3 us

profile of v16, /device:TPU:1, one launch (start us, length us, event | category | flops | bytes accessed | tf_op | source)
XLA Modules:
  0.0 132.3 jit_solution(10382127373007693885)
XLA Ops:
  0.6 1.8 %copy.8.head_ref = bf16[128,1000]{1,0:T(8,128)(2,1)} copy(bf16[128,1000]{0,1:T(8,128)(2,1)} %param.10) | data formatting | bytes 512000 | tf_op args[4]
  2.5 1.3 broadcast_in_dim.25
  3.8 84.1 %shard_map.77 = (bf16[768,4096]{1,0:T(8,128)(2,1)}, bf16[4,8,128,1000]{3,2,1,0:T(8,128)(2,1)}) custom-call(bf16[768,256]{1,0:T(8,128)(2,1)} %rows_ref.1, bf16[128,1000]{1,0:T(8,128)(2,1)} %copy.8.head_ref, f32[1,4096]{1,0:T(1,128)} %bitcast.10), custom_call_target="tpu_custom_call" | custom-call | tf_op jit(solution)/shard_map/pallas_call | solution.py:300
  87.8 0.0 copy-start
  87.8 11.3 %fusion.12 = (f32[768]{0:T(1024)S(1)}, f32[768,1000]{0,1:T(8,128)S(1)}) fusion(bf16[768,4096]{1,0:T(8,128)(2,1)} %get-tuple-element.4, bf16[4096,1000]{1,0:T(8,128)(2,1)} %bitcast.11), kind=kOutput, calls=%fused_computation.27 | convolution fusion | flops 6292222976 | bytes 17558528 | tf_op jit(solution)/shard_map/dot_general | solution.py:318
  99.1 0.0 copy-start.1
  99.1 0.0 copy-done
  99.1 1.4 %fusion = (f32[768]{0:T(1024)S(1)}, f32[768]{0:T(1024)S(1)}, f32[768]{0:T(1024)S(1)}) fusion(f32[768,1000]{0,1:T(8,128)S(1)} %get-tuple-element.16, f32[768]{0:T(1024)S(1)} %get-tuple-element.15, s32[768]{0:T(1024)S(1)} %copy-done, s32[1000]{0:T(1024)S(1)} %iota_add_fusion), kind=kLoop, calls=%fused_computation.3 | loop fusion | flops 5373696 | bytes 3091360 | tf_op jit(solution)/shard_map/reduce_sum | solution.py:321
  100.6 0.6 pad_maximum_fusion.stats_ref
  101.8 27.9 %shard_map.78 = f32[32,2,768]{2,1,0:T(2,128)} custom-call(f32[4,768]{1,0:T(4,128)} %pad_maximum_fusion.stats_ref, s32[1,1]{1,0:T(1,128)} %bitcast.7.count_ref), custom_call_target="tpu_custom_call" | custom-call | tf_op jit(solution)/shard_map/pallas_call | solution.py:76
  129.7 1.2 fusion.11
  130.9 0.0 copy-done.1
  130.9 0.7 fusion.1
  131.7 0.7 fusion.2
  (6 shorter events, 0.0 us)
Async XLA Ops:
  87.8 11.3 %copy-start = (s32[768]{0:T(1024)S(1)}, s32[768]{0:T(1024)}, u32[]{:S(2)}) copy-start(s32[768]{0:T(1024)} %param.7) | copy-start | bytes 9220
  99.1 31.8 %copy-start.1 = (s32[768]{0:T(1024)S(1)}, s32[768]{0:T(1024)}, u32[]{:S(2)}) copy-start(s32[768]{0:T(1024)} %param.11) | copy-start | bytes 9220

commit v17 on v14

--- a/solution.py
+++ b/solution.py
@@ -12,7 +12,8 @@
 EPSILON = 1e-05
 
 
-def _exchange_kernel(n_voc, n_grp, stats_ref, count_ref, out_ref, parts, voc_sems, grp_sems):
+def _exchange_kernel(n_voc, n_grp, peak_ref, total_ref, weighted_ref, picked_ref, count_ref, out_ref,
+                     mine, parts, voc_sems, grp_sems):
     g = lax.axis_index("grp")
     v = lax.axis_index("voc")
 
@@ -50,10 +51,13 @@
         for copy in copies:
             copy.wait_send()
 
+    for i, ref in enumerate((peak_ref, total_ref, weighted_ref, picked_ref)):
+        mine[pl.ds(i, 1), :] = ref[...]
+
     def keep_stats():
-        parts[v] = stats_ref[...]
-
-    send_all(stats_ref, parts, v, n_voc, voc_sems, along_voc, keep_stats)
+        parts[v] = mine[...]
+
+    send_all(mine, parts, v, n_voc, voc_sems, along_voc, keep_stats)
     every = parts[...]
     quarter = every.shape[1] // 4
     peaks = every[:, :quarter]
@@ -72,16 +76,17 @@
 
 
 def exchange(stats, count, n_voc, n_grp):
-    rows, lanes = stats.shape
+    rows, lanes = len(stats), stats[0].shape[1]
+    dtype = stats[0].dtype
     return pl.pallas_call(
         functools.partial(_exchange_kernel, n_voc, n_grp),
-        out_shape=jax.ShapeDtypeStruct((n_grp, rows // 2, lanes), stats.dtype),
-        in_specs=[pl.BlockSpec(memory_space=pltpu.VMEM)] * 2,
+        out_shape=jax.ShapeDtypeStruct((n_grp, rows // 2, lanes), dtype),
+        in_specs=[pl.BlockSpec(memory_space=pltpu.VMEM)] * (rows + 1),
         out_specs=pl.BlockSpec(memory_space=pltpu.VMEM),
-        scratch_shapes=[pltpu.VMEM((n_voc, rows, lanes), stats.dtype),
+        scratch_shapes=[pltpu.VMEM((rows, lanes), dtype), pltpu.VMEM((n_voc, rows, lanes), dtype),
                         pltpu.SemaphoreType.DMA((2, n_voc)), pltpu.SemaphoreType.DMA((2, n_grp))],
         compiler_params=pltpu.CompilerParams(collective_id=0, has_side_effects=True),
-    )(stats, count)
+    )(*stats, count)
 
 
 class _Ring:
@@ -297,7 +302,7 @@
     weighted = jnp.sum(shifted * logits, axis=1)
     global_columns = lax.axis_index("voc") * vocab_local + jnp.arange(vocab_local, dtype=jnp.int32)
     picked = jnp.sum(jnp.where(global_columns[None, :] == targets[:, None], logits, 0.0), axis=1)
-    stats = jnp.stack([peak, total, weighted, picked])
+    stats = [part[None, :] for part in (peak, total, weighted, picked)]
     results = exchange(stats, row_count.reshape(1, 1), n_voc, n_grp).reshape(n_grp, 2, tok_rows)
     lanes = 128
     every = jnp.concatenate(

time: 126 us -> 128 us (1.016)
  local copies, waits for them, and re-layouts: 3.05 us -> 5.36 us
    broadcast_in_dim x0 -> x4, local copies, waits for them, and re-layouts: none -> 2.33 us  [local(): stats = [part[None, :] for part in (peak, total, weighted, picked)]]
where the time goes in v17:
time: 128 us; the launch traced here: 127 us
  Pallas kernels  105 us (82%)
  matrix products  11.9 us (9%)
  local copies, waits for them, and re-layouts  5.36 us (4%)
  other arithmetic  3.36 us (3%)
  between operations  1.38 us (1%)
    pallas_call x1, Pallas kernels, gather_both(): pl.pallas_call(functools.partial(_gather_kernel, n_x, n_z, n_y), out_shap...  79.1 us
    pallas_call x1, Pallas kernels, exchange(): pl.pallas_call(functools.partial(_exchange_kernel, n_voc, n_grp), out_sha...  26.2 us
    dot_general x1, matrix products, local(): logits = jnp.dot(normed, piece, preferred_element_type=jnp.float32)  11.2 us

profile of v17, /device:TPU:1, one launch (start us, length us, event | category | flops | bytes accessed | tf_op | source)
XLA Modules:
  0.0 127.3 jit_solution(9519010530681785966)
XLA Ops:
  0.6 1.8 %copy.8.head_ref = bf16[128,1000]{1,0:T(8,128)(2,1)} copy(bf16[128,1000]{0,1:T(8,128)(2,1)} %param.10) | data formatting | bytes 512000 | tf_op args[4]
  2.5 1.3 %broadcast_in_dim.41 = f32[4096]{0:T(1024)} convert(bf16[4096]{0:T(1024)(128)(2,1)} %param.9) | non-fusion elementwise | flops 4096 | bytes 24576 | tf_op jit(solution)/shard_map/broadcast_in_dim | solution.py:279
  3.8 79.1 %shard_map.77 = (bf16[768,4096]{1,0:T(8,128)(2,1)}, bf16[4,8,128,1000]{3,2,1,0:T(8,128)(2,1)}) custom-call(bf16[768,256]{1,0:T(8,128)(2,1)} %rows_ref.1, bf16[128,1000]{1,0:T(8,128)(2,1)} %copy.8.head_ref, f32[1,4096]{1,0:T(1,128)} %bitcast.10), custom_call_target="tpu_custom_call" | custom-call | tf_op jit(solution)/shard_map/pallas_call | solution.py:280
  82.8 0.0 copy-start
  82.8 11.2 %fusion.12 = (f32[768]{0:T(1024)S(1)}, f32[768,1000]{0,1:T(8,128)S(1)}) fusion(bf16[768,4096]{1,0:T(8,128)(2,1)} %get-tuple-element.4, bf16[4096,1000]{1,0:T(8,128)(2,1)} %bitcast.11), kind=kOutput, calls=%fused_computation.26 | convolution fusion | flops 6292222976 | bytes 17558528 | tf_op jit(solution)/shard_map/dot_general | solution.py:298
  94.1 0.0 copy-start.1
  94.1 0.0 copy-done
  94.1 1.4 %multiply_reduce_fusion = (f32[768]{0:T(1024)S(1)}, f32[768]{0:T(1024)S(1)}, f32[768]{0:T(1024)S(1)}) fusion(f32[768,1000]{0,1:T(8,128)S(1)} %get-tuple-element.16, f32[768]{0:T(1024)S(1)} %get-tuple-element.15, s32[768]{0:T(1024)S(1)} %copy-done, s32[1000]{0:T(1024)S(1)} %iota_add_fusion), kind=kLoop, calls=%fused_computation.1 | loop fusion | flops 5373696 | bytes 3091360 | tf_op jit(solution)/shard_map/reduce_sum | solution.py:302
  95.5 0.6 broadcast_in_dim.36.total_ref
  96.1 0.6 broadcast_in_dim.37.weighted_ref
  96.7 0.6 broadcast_in_dim.39.picked_ref
  97.3 0.6 broadcast_in_dim.35.peak_ref
  98.5 26.2 %shard_map.78 = f32[32,2,768]{2,1,0:T(2,128)} custom-call(f32[1,768]{1,0:T(1,128)} %broadcast_in_dim.35.peak_ref, f32[1,768]{1,0:T(1,128)} %broadcast_in_dim.36.total_ref, f32[1,768]{1,0:T(1,128)} %broadcast_in_dim.37.weighted_ref, f32[1,768]{1,0:T(1,128)} %broadcast_in_dim.39.picked_ref, s32[1,1]{1,0:T(1,128)} %bitcast.7.count_ref), custom_call_target="tpu_custom_call" | custom-call | tf_op jit(solution)/shard_map/pallas_call | solution.py:81
  124.7 1.2 fusion.11
  125.9 0.0 copy-done.1
  125.9 0.7 fusion.1
  126.6 0.7 fusion.2
  (2 shorter events, 0.0 us)
Async XLA Ops:
  82.8 11.3 %copy-start = (s32[768]{0:T(1024)S(1)}, s32[768]{0:T(1024)}, u32[]{:S(2)}) copy-start(s32[768]{0:T(1024)} %param.7) | copy-start | bytes 9220
  94.1 31.8 %copy-start.1 = (s32[768]{0:T(1024)S(1)}, s32[768]{0:T(1024)}, u32[]{:S(2)}) copy-start(s32[768]{0:T(1024)} %param.11) | copy-start | bytes 9220

commit v18 on v14

--- a/solution.py
+++ b/solution.py
@@ -203,7 +203,8 @@
     copy = to_partner(rows_ref, y)
     copy.start()
     pair_copies.append(copy)
-    rows_out[:, cols(v)] = rows_ref[...]
+    own_rows = pltpu.make_async_copy(rows_ref, rows_out.at[:, cols(v)], local_sem.at[1])
+    own_rows.start()
     def halves(size, start=0):
         return lambda part: pl.ds(start, size) if part is None else pl.ds(start + part * (size // 2), size // 2)
 
@@ -248,6 +249,7 @@
             send_sem=pair_sems.at[0, t], recv_sem=pair_sems.at[1, t],
             device_id=(me, partner), device_id_type=MESH,
         ).wait_recv()
+    own_rows.wait()
     chunk = 64
 
     def norm_chunk(i, carry):
@@ -279,7 +281,7 @@
         in_specs=[pl.BlockSpec(memory_space=pltpu.VMEM)] * 3,
         out_specs=(pl.BlockSpec(memory_space=pltpu.VMEM), pl.BlockSpec(memory_space=pltpu.VMEM)),
         scratch_shapes=[pltpu.VMEM((rows, width * n_voc), hidden.dtype),
-                        pltpu.SemaphoreType.DMA((1,)), pltpu.SemaphoreType.DMA((5, 4, steps)),
+                        pltpu.SemaphoreType.DMA((2,)), pltpu.SemaphoreType.DMA((5, 4, steps)),
                         pltpu.SemaphoreType.DMA((2, n_y))],
         compiler_params=pltpu.CompilerParams(collective_id=3, has_side_effects=True),
     )(hidden, piece, gain)

time: 126 us -> 126 us (level)
  no operation moved by 1% of the time
where the time goes in v18:
time: 126 us
  Pallas kernels  105 us (83%)
  matrix products  12 us (10%)
  other arithmetic  3.97 us (3%)
  local copies, waits for them, and re-layouts  3.05 us (2%)
  between operations  1.41 us (1%)
    pallas_call x1, Pallas kernels, gather_both(): pl.pallas_call(functools.partial(_gather_kernel, n_x, n_z, n_y), out_shap...  79 us
    pallas_call x1, Pallas kernels, exchange(): pl.pallas_call(functools.partial(_exchange_kernel, n_voc, n_grp), out_sha...  26.3 us
    dot_general x1, matrix products, local(): logits = jnp.dot(normed, piece, preferred_element_type=jnp.float32)  11.3 us

profile of v18, /device:TPU:1, one launch (start us, length us, event | category | flops | bytes accessed | tf_op | source)
XLA Modules:
  0.0 125.7 jit_solution(7566168906271742281)
XLA Ops:
  0.6 1.8 %copy.8.head_ref = bf16[128,1000]{1,0:T(8,128)(2,1)} copy(bf16[128,1000]{0,1:T(8,128)(2,1)} %param.10) | data formatting | bytes 512000 | tf_op args[4]
  2.5 1.3 %broadcast_in_dim.25 = f32[4096]{0:T(1024)} convert(bf16[4096]{0:T(1024)(128)(2,1)} %param.9) | non-fusion elementwise | flops 4096 | bytes 24576 | tf_op jit(solution)/shard_map/broadcast_in_dim | solution.py:276
  3.8 79.0 %shard_map.77 = (bf16[768,4096]{1,0:T(8,128)(2,1)}, bf16[4,8,128,1000]{3,2,1,0:T(8,128)(2,1)}) custom-call(bf16[768,256]{1,0:T(8,128)(2,1)} %rows_ref.1, bf16[128,1000]{1,0:T(8,128)(2,1)} %copy.8.head_ref, f32[1,4096]{1,0:T(1,128)} %bitcast.10), custom_call_target="tpu_custom_call" | custom-call | tf_op jit(solution)/shard_map/pallas_call | solution.py:277
  82.8 0.0 copy-start
  82.8 11.3 %fusion.12 = (f32[768]{0:T(1024)S(1)}, f32[768,1000]{0,1:T(8,128)S(1)}) fusion(bf16[768,4096]{1,0:T(8,128)(2,1)} %get-tuple-element.4, bf16[4096,1000]{1,0:T(8,128)(2,1)} %bitcast.11), kind=kOutput, calls=%fused_computation.27 | convolution fusion | flops 6292222976 | bytes 17558528 | tf_op jit(solution)/shard_map/dot_general | solution.py:295
  94.1 0.0 copy-start.1
  94.1 0.0 copy-done
  94.1 1.4 %fusion = (f32[768]{0:T(1024)S(1)}, f32[768]{0:T(1024)S(1)}, f32[768]{0:T(1024)S(1)}) fusion(f32[768,1000]{0,1:T(8,128)S(1)} %get-tuple-element.16, f32[768]{0:T(1024)S(1)} %get-tuple-element.15, s32[768]{0:T(1024)S(1)} %copy-done, s32[1000]{0:T(1024)S(1)} %iota_add_fusion), kind=kLoop, calls=%fused_computation.3 | loop fusion | flops 5373696 | bytes 3091360 | tf_op jit(solution)/shard_map/reduce_sum | solution.py:298
  95.5 0.6 pad_maximum_fusion.stats_ref
  96.8 26.3 %shard_map.78 = f32[32,2,768]{2,1,0:T(2,128)} custom-call(f32[4,768]{1,0:T(4,128)} %pad_maximum_fusion.stats_ref, s32[1,1]{1,0:T(1,128)} %bitcast.7.count_ref), custom_call_target="tpu_custom_call" | custom-call | tf_op jit(solution)/shard_map/pallas_call | solution.py:76
  123.1 1.2 fusion.11
  124.3 0.0 copy-done.1
  124.3 0.7 fusion.1
  125.0 0.7 fusion.2
  (6 shorter events, 0.0 us)
Async XLA Ops:
  82.8 11.3 %copy-start = (s32[768]{0:T(1024)S(1)}, s32[768]{0:T(1024)}, u32[]{:S(2)}) copy-start(s32[768]{0:T(1024)} %param.7) | copy-start | bytes 9220
  94.1 30.2 %copy-start.1 = (s32[768]{0:T(1024)S(1)}, s32[768]{0:T(1024)}, u32[]{:S(2)}) copy-start(s32[768]{0:T(1024)} %param.11) | copy-start | bytes 9220

commit v19 on v14

--- a/solution.py
+++ b/solution.py
@@ -216,9 +216,9 @@
                     lambda p: head_ref.at[lo_part(p)], sems.at[0])
     first_z = _Ring(z, n_z, along_z, lambda t, p=None: head_out.at[x, t, hi_part(p)],
                     lambda p: head_ref.at[hi_part(p)], sems.at[1])
-    rows.advance()
     first_x.advance()
     first_z.advance()
+    rows.advance()
     first_x.advance()
     first_z.advance()
     own.wait()

time: 126 us -> 126 us (level)
  no operation moved by 1% of the time
where the time goes in v19:
time: 126 us
  Pallas kernels  105 us (83%)
  matrix products  12 us (10%)
  other arithmetic  3.97 us (3%)
  local copies, waits for them, and re-layouts  3.05 us (2%)
  between operations  1.41 us (1%)
    pallas_call x1, Pallas kernels, gather_both(): pl.pallas_call(functools.partial(_gather_kernel, n_x, n_z, n_y), out_shap...  79.1 us
    pallas_call x1, Pallas kernels, exchange(): pl.pallas_call(functools.partial(_exchange_kernel, n_voc, n_grp), out_sha...  26.2 us
    dot_general x1, matrix products, local(): logits = jnp.dot(normed, piece, preferred_element_type=jnp.float32)  11.2 us

profile of v19, /device:TPU:1, one launch (start us, length us, event | category | flops | bytes accessed | tf_op | source)
XLA Modules:
  0.0 125.7 jit_solution(11611247344446536238)
XLA Ops:
  0.6 1.8 %copy.8.head_ref = bf16[128,1000]{1,0:T(8,128)(2,1)} copy(bf16[128,1000]{0,1:T(8,128)(2,1)} %param.10) | data formatting | bytes 512000 | tf_op args[4]
  2.5 1.3 %broadcast_in_dim.25 = f32[4096]{0:T(1024)} convert(bf16[4096]{0:T(1024)(128)(2,1)} %param.9) | non-fusion elementwise | flops 4096 | bytes 24576 | tf_op jit(solution)/shard_map/broadcast_in_dim | solution.py:274
  3.8 79.1 %shard_map.77 = (bf16[768,4096]{1,0:T(8,128)(2,1)}, bf16[4,8,128,1000]{3,2,1,0:T(8,128)(2,1)}) custom-call(bf16[768,256]{1,0:T(8,128)(2,1)} %rows_ref.1, bf16[128,1000]{1,0:T(8,128)(2,1)} %copy.8.head_ref, f32[1,4096]{1,0:T(1,128)} %bitcast.10), custom_call_target="tpu_custom_call" | custom-call | tf_op jit(solution)/shard_map/pallas_call | solution.py:275
  82.8 0.0 copy-start
  82.8 11.2 %fusion.12 = (f32[768]{0:T(1024)S(1)}, f32[768,1000]{0,1:T(8,128)S(1)}) fusion(bf16[768,4096]{1,0:T(8,128)(2,1)} %get-tuple-element.4, bf16[4096,1000]{1,0:T(8,128)(2,1)} %bitcast.11), kind=kOutput, calls=%fused_computation.27 | convolution fusion | flops 6292222976 | bytes 17558528 | tf_op jit(solution)/shard_map/dot_general | solution.py:293
  94.1 0.0 copy-start.1
  94.1 0.0 copy-done
  94.1 1.4 %fusion = (f32[768]{0:T(1024)S(1)}, f32[768]{0:T(1024)S(1)}, f32[768]{0:T(1024)S(1)}) fusion(f32[768,1000]{0,1:T(8,128)S(1)} %get-tuple-element.16, f32[768]{0:T(1024)S(1)} %get-tuple-element.15, s32[768]{0:T(1024)S(1)} %copy-done, s32[1000]{0:T(1024)S(1)} %iota_add_fusion), kind=kLoop, calls=%fused_computation.3 | loop fusion | flops 5373696 | bytes 3091360 | tf_op jit(solution)/shard_map/reduce_sum | solution.py:296
  95.6 0.6 pad_maximum_fusion.stats_ref
  96.8 26.2 %shard_map.78 = f32[32,2,768]{2,1,0:T(2,128)} custom-call(f32[4,768]{1,0:T(4,128)} %pad_maximum_fusion.stats_ref, s32[1,1]{1,0:T(1,128)} %bitcast.7.count_ref), custom_call_target="tpu_custom_call" | custom-call | tf_op jit(solution)/shard_map/pallas_call | solution.py:76
  123.0 1.2 fusion.11
  124.2 0.0 copy-done.1
  124.3 0.7 fusion.1
  125.0 0.7 fusion.2
  (6 shorter events, 0.0 us)
Async XLA Ops:
  82.8 11.3 %copy-start = (s32[768]{0:T(1024)S(1)}, s32[768]{0:T(1024)}, u32[]{:S(2)}) copy-start(s32[768]{0:T(1024)} %param.7) | copy-start | bytes 9220
  94.1 30.1 %copy-start.1 = (s32[768]{0:T(1024)S(1)}, s32[768]{0:T(1024)}, u32[]{:S(2)}) copy-start(s32[768]{0:T(1024)} %param.11) | copy-start | bytes 9220
